TPU v7x, 32 devices: a whole 2x2x4 slice. The times are simulated.
32 devices in a mesh: maps: 2 (over x), row: 4 (over y, core), col: 4 (over z).
Axes of the slice: x: 2, y: 2, z: 4, core: 2. Of those that a mesh axis runs over, the one named last changes fastest.
Arguments:
- shear: float32 [2, 2, 2048, 2048], P(None, 'maps', 'row', 'col'), parts along dimension 1, may hold values from -600 to 600
- smoothing: float32 [2], P('maps'), parts along dimension 0, may hold values from 0.6 to 1.2
- offsets: int32 [2, 128, 128], P('maps', ('row', 'col')), parts along dimension 0, may hold values from 0 to 255
- thresholds: int32 [2, 16], P('maps'), parts along dimension 0, may hold values from -4 to 19
Outputs:
- snr: float32 [2, 2048, 2048], P('maps', ('row', 'col')), parts along dimension 0
- heights: float32 [2, 128, 128], P('maps', ('row', 'col')), parts along dimension 0
- counts: float32 [2, 16], P('maps'), parts along dimension 0
There are 2 independent parts, one for each index of `maps`. A program takes and returns all parts, laid end to end along the dimension named above; each array names one. Nothing has to cross between parts.
All inputs are finite; a program needn't handle non-finite values.
Results may differ from a plain program's by a relative error of at most 0.00014.
Values sent between devices are 32-bit elements; how exact they have to be, the bound alone decides.
A program may use at most 64 MiB of HBM per device.

v0:
```python
from functools import partial
import math

import jax
import jax.numpy as jnp
from jax import lax
from jax.sharding import PartitionSpec as P

NX = 2048
NY = 2048
RADIX = 16
CELL = 16


HIGH = lax.Precision.HIGHEST
peak_soft = 0.05
bin_soft = 0.1
bin_step = 0.25


def with_halo(x, sides, width):
    for axis, dim in sides:
        size, length = (lax.axis_size(axis), x.shape[dim])
        up = [(i, (i + 1) % size) for i in range(size)]
        down = [(j, i) for i, j in up]
        last = lax.slice_in_dim(x, length - width, length, axis=dim)
        initial = lax.slice_in_dim(x, 0, width, axis=dim)
        before = lax.ppermute(last, axis, up)
        after = lax.ppermute(initial, axis, down)
        x = jnp.concatenate([before, x, after], axis=dim)
    return x


def table(rows, cols, length, sign):
    left = jnp.arange(rows, dtype=jnp.int32)[:, None]
    right = jnp.arange(cols, dtype=jnp.int32)[None, :]
    angle = sign * 2.0 * math.pi / length * (left * right % length).astype(jnp.float32)
    return (jnp.cos(angle), jnp.sin(angle))


def cform(form, left, right):
    apply = partial(jnp.einsum, form, precision=HIGH)
    return (
        apply(left[0], right[0]) - apply(left[1], right[1]),
        apply(left[0], right[1]) + apply(left[1], right[0]),
    )


def cmul(left, right):
    return (left[0] * right[0] - left[1] * right[1], left[0] * right[1] + left[1] * right[0])


def forward_last(real_part, imag_part):
    lead = real_part.shape[:-1]
    length = real_part.shape[-1]
    inner = length // RADIX
    part = (real_part.reshape(lead + (RADIX, inner)), imag_part.reshape(lead + (RADIX, inner)))
    part = cform("kn,...ni->...ki", table(RADIX, RADIX, RADIX, -1), part)
    part = cmul(part, table(RADIX, inner, length, -1))
    part = cform("...ki,il->...kl", part, table(inner, inner, inner, -1))
    return (part[0].reshape(lead + (length,)), part[1].reshape(lead + (length,)))


def forward_middle(real_part, imag_part):
    maps, length, cols = real_part.shape
    inner = length // RADIX
    part = (
        real_part.reshape(maps, RADIX, inner, cols),
        imag_part.reshape(maps, RADIX, inner, cols),
    )
    part = cform("kn,mniy->mkiy", table(RADIX, RADIX, RADIX, -1), part)
    twist = table(RADIX, inner, length, -1)
    part = cmul(part, (twist[0][:, :, None], twist[1][:, :, None]))
    part = cform("mkiy,il->mkly", part, table(inner, inner, inner, -1))
    return (part[0].reshape(maps, length, cols), part[1].reshape(maps, length, cols))


def inverse_middle(real_part, imag_part):
    maps, length, cols = real_part.shape
    inner = length // RADIX
    part = (
        real_part.reshape(maps, RADIX, inner, cols),
        imag_part.reshape(maps, RADIX, inner, cols),
    )
    part = cform("mkjy,jn->mkny", part, table(inner, inner, inner, 1))
    twist = table(RADIX, inner, length, 1)
    part = cmul(part, (twist[0][:, :, None], twist[1][:, :, None]))
    part = cform("nk,mkiy->mniy", table(RADIX, RADIX, RADIX, 1), part)
    return (
        part[0].reshape(maps, length, cols) / length,
        part[1].reshape(maps, length, cols) / length,
    )


def inverse_last_real(real_part, imag_part):
    lead = real_part.shape[:-1]
    length = real_part.shape[-1]
    inner = length // RADIX
    part = (real_part.reshape(lead + (RADIX, inner)), imag_part.reshape(lead + (RADIX, inner)))
    part = cform("...kj,jn->...kn", part, table(inner, inner, inner, 1))
    part = cmul(part, table(RADIX, inner, length, 1))
    outer = table(RADIX, RADIX, RADIX, 1)
    real = jnp.einsum("nk,...ki->...ni", outer[0], part[0], precision=HIGH) - jnp.einsum(
        "nk,...ki->...ni", outer[1], part[1], precision=HIGH
    )
    return real.reshape(lead + (length,)) / length


def signed_frequency(flat, length):
    inner = length // RADIX
    freq = flat // inner + RADIX * (flat % inner)
    return jnp.where(freq < length // 2, freq, freq - length).astype(jnp.float32)


def apply_kernel(real_part, imag_part, smoothing):
    maps, length, cols = real_part.shape
    total = cols * lax.axis_size(("row", "col"))
    freq_x = signed_frequency(jnp.arange(length, dtype=jnp.int32), length)[:, None]
    freq_y = signed_frequency(
        lax.axis_index(("row", "col")) * cols + jnp.arange(cols, dtype=jnp.int32), total
    )[None, :]
    square = jnp.maximum(freq_x * freq_x + freq_y * freq_y, 1.0)
    width = smoothing[:, None, None]
    damp = jnp.exp(
        -2.0 * math.pi**2 * width * width * ((freq_x / length) ** 2 + (freq_y / total) ** 2)
    )
    kernel = (
        (freq_x * freq_x - freq_y * freq_y) / square * damp,
        -2.0 * freq_x * freq_y / square * damp,
    )
    return cmul((real_part, imag_part), kernel)


def spectral_pass(real_part, imag_part, smoothing):
    real_part, imag_part = (
        lax.all_to_all(real_part, "col", split_axis=1, concat_axis=2, tiled=True),
        lax.all_to_all(imag_part, "col", split_axis=1, concat_axis=2, tiled=True),
    )
    real_part, imag_part = forward_last(real_part, imag_part)
    real_part, imag_part = (
        lax.all_to_all(real_part, ("row", "col"), split_axis=2, concat_axis=1, tiled=True),
        lax.all_to_all(imag_part, ("row", "col"), split_axis=2, concat_axis=1, tiled=True),
    )
    real_part, imag_part = forward_middle(real_part, imag_part)
    real_part, imag_part = apply_kernel(real_part, imag_part, smoothing)
    real_part, imag_part = inverse_middle(real_part, imag_part)
    real_part, imag_part = (
        lax.all_to_all(real_part, ("row", "col"), split_axis=1, concat_axis=2, tiled=True),
        lax.all_to_all(imag_part, ("row", "col"), split_axis=1, concat_axis=2, tiled=True),
    )
    return inverse_last_real(real_part, imag_part)


def body(shear, smoothing, offsets, thresholds):
    kappa = spectral_pass(shear[0], shear[1], smoothing)
    maps, rows, width = kappa.shape
    padded = with_halo(kappa, ((("row", "col"), 1),), 1)
    nearest = None
    for step_row in range(3):
        band = padded[:, step_row : step_row + rows]
        for step_col in (-1, 0, 1):
            if step_row == 1 and step_col == 0:
                continue
            moved = jnp.roll(band, step_col, axis=2)
            nearest = moved if nearest is None else jnp.maximum(nearest, moved)
    height_map = kappa - nearest
    full = jnp.repeat(jnp.repeat(offsets, CELL, axis=1), CELL, axis=2)
    code = (jnp.arange(rows, dtype=jnp.int32) % CELL)[:, None] * CELL + (
        jnp.arange(width, dtype=jnp.int32) % CELL
    )[None, :]
    chosen = full == code[None]
    blocks = (
        jnp.arange(width, dtype=jnp.int32)[:, None] // CELL
        == jnp.arange(width // CELL, dtype=jnp.int32)[None, :]
    ).astype(jnp.float32)

    def pick(values):
        picked = jnp.where(chosen, values, 0.0)
        summed = picked.reshape(maps, rows // CELL, CELL, width).sum(axis=2)
        return jnp.einsum("mxy,yc->mxc", summed, blocks, precision=HIGH)

    total = lax.psum(jnp.sum(kappa * kappa, axis=(1, 2)), ("row", "col"))
    rms = jnp.sqrt(total / (NX * NY) + 1e-06)
    snr = kappa / rms[:, None, None]
    heights = pick(height_map) / rms[:, None, None]
    values = pick(kappa) / rms[:, None, None]
    weight = jax.nn.sigmoid(heights / peak_soft)
    levels = bin_step * thresholds.astype(jnp.float32)
    above = jax.nn.sigmoid((values[..., None] - levels[:, None, None, :]) / bin_soft)
    local = jnp.sum(weight[..., None] * above, axis=(1, 2))
    counts = lax.psum(local, ("row", "col"))
    return (snr, heights, counts)


def solution(mesh):
    return jax.shard_map(
        body,
        mesh=mesh,
        in_specs=(
            P(None, "maps", "row", "col"),
            P("maps"),
            P("maps", ("row", "col"), None),
            P("maps", None),
        ),
        out_specs=(
            P("maps", ("row", "col"), None),
            P("maps", ("row", "col"), None),
            P("maps", None),
        ),
        check_vma=False,
    )
```

profile of v0, /device:TPU:0, one launch (start us, length us, event | category | flops | bytes accessed | tf_op | source)
XLA Modules:
  0.0 312.4 jit_solution(14847953061631260756)
XLA Ops:
  0.6 1.7 fusion.319
  2.3 2.0 copy.297
  4.4 6.3 %all-to-all-start.1 = ((f32[1,512,512]{2,0,1:T(1,128)}), f32[1,512,512]{2,0,1:T(1,128)S(1)}, u32[]{:S(2)}, u32[]{:S(2)}) async-start(f32[1,512,512]{2,0,1:T(1,128)} %bitcast.246), calls=%async_computation.1 | async-start | bytes 2097152 | tf_op jit(solution)/shard_map/all_to_all | solution.py:137
  10.7 2.1 copy.298
  12.8 23.7 %all-to-all-done.1 = f32[1,512,512]{2,0,1:T(1,128)S(1)} async-done(((f32[1,512,512]{2,0,1:T(1,128)}), f32[1,512,512]{2,0,1:T(1,128)S(1)}, u32[]{:S(2)}, u32[]{:S(2)}) %all-to-all-start.1) | async-done | bytes 1048608 | tf_op jit(solution)/shard_map/all_to_all | solution.py:137
  36.5 3.7 %all-to-all-start = ((f32[1,512,512]{2,0,1:T(1,128)}), f32[1,512,512]{2,0,1:T(1,128)S(1)}, u32[]{:S(2)}, u32[]{:S(2)}) async-start(f32[1,512,512]{2,0,1:T(1,128)} %bitcast.247), calls=%async_computation | async-start | bytes 2097152 | tf_op jit(solution)/shard_map/all_to_all | solution.py:136
  41.3 1.0 fusion.138
  42.4 23.0 %all-to-all-done = f32[1,512,512]{2,0,1:T(1,128)S(1)} async-done(((f32[1,512,512]{2,0,1:T(1,128)}), f32[1,512,512]{2,0,1:T(1,128)S(1)}, u32[]{:S(2)}, u32[]{:S(2)}) %all-to-all-start) | async-done | bytes 1048608 | tf_op jit(solution)/shard_map/all_to_all | solution.py:136
  65.4 1.6 copy.300
  67.1 1.6 reshape.873
  68.7 1.0 fusion.140
  69.8 1.0 fusion.11
  70.8 1.3 add_bitcast_fusion.2
  72.1 1.6 fusion.58
  73.7 2.6 convolution_add_fusion.5
  76.2 4.2 %all-to-all-start.3 = ((f32[1,128,2048]{1,0,2:T(1,128)}), f32[1,128,2048]{1,0,2:T(1,128)S(1)}, u32[]{:S(2)}, u32[]{:S(2)}) async-start(f32[1,128,2048]{1,0,2:T(1,128)} %bitcast.32), calls=%async_computation.3 | async-start | bytes 2097152 | tf_op jit(solution)/shard_map/all_to_all | solution.py:142
  80.4 1.6 fusion.60
  82.0 2.6 convolution_subtract_fusion.6
  84.6 22.7 %all-to-all-done.3 = f32[1,128,2048]{1,0,2:T(1,128)S(1)} async-done(((f32[1,128,2048]{1,0,2:T(1,128)}), f32[1,128,2048]{1,0,2:T(1,128)S(1)}, u32[]{:S(2)}, u32[]{:S(2)}) %all-to-all-start.3) | async-done | bytes 1048608 | tf_op jit(solution)/shard_map/all_to_all | solution.py:142
  107.3 3.7 %all-to-all-start.2 = ((f32[1,128,2048]{1,0,2:T(1,128)}), f32[1,128,2048]{1,0,2:T(1,128)S(1)}, u32[]{:S(2)}, u32[]{:S(2)}) async-start(f32[1,128,2048]{1,0,2:T(1,128)} %bitcast.25), calls=%async_computation.2 | async-start | bytes 2097152 | tf_op jit(solution)/shard_map/all_to_all | solution.py:141
  111.9 1.7 copy.253
  113.7 1.1 fusion.37
  114.8 23.0 %all-to-all-done.2 = f32[1,128,2048]{1,0,2:T(1,128)S(1)} async-done(((f32[1,128,2048]{1,0,2:T(1,128)}), f32[1,128,2048]{1,0,2:T(1,128)S(1)}, u32[]{:S(2)}, u32[]{:S(2)}) %all-to-all-start.2) | async-done | bytes 1048608 | tf_op jit(solution)/shard_map/all_to_all | solution.py:141
  137.8 1.0 copy-done.2
  138.7 1.7 copy.250
  140.5 1.1 fusion.35
  141.5 1.1 fusion.9
  142.6 1.5 add_bitcast_fusion.1
  144.1 1.5 fusion.52
  145.7 1.5 fusion.54
  147.2 1.5 fusion.7
  148.7 1.6 fusion.8
  150.2 2.2 fusion.30
  152.5 2.0 fusion.32
  154.5 2.1 fusion.5
  156.6 2.5 add_bitcast_fusion
  159.1 1.6 fusion.48
  160.7 1.6 fusion.4
  162.4 1.3 copy.214
  163.7 3.9 %all-to-all-start.4 = ((f32[1,2048,128]{2,0,1:T(1,128)}), f32[1,2048,128]{2,0,1:T(1,128)S(1)}, u32[]{:S(2)}, u32[]{:S(2)}) async-start(f32[1,2048,128]{2,0,1:T(1,128)} %bitcast.262), calls=%async_computation.4 | async-start | bytes 2097152 | tf_op jit(solution)/shard_map/all_to_all | solution.py:148
  167.6 1.6 fusion.44
  169.2 1.6 fusion.2
  170.8 1.4 copy.218
  172.2 22.1 %all-to-all-done.4 = f32[1,2048,128]{2,0,1:T(1,128)S(1)} async-done(((f32[1,2048,128]{2,0,1:T(1,128)}), f32[1,2048,128]{2,0,1:T(1,128)S(1)}, u32[]{:S(2)}, u32[]{:S(2)}) %all-to-all-start.4) | async-done | bytes 1048608 | tf_op jit(solution)/shard_map/all_to_all | solution.py:148
  194.4 3.7 %all-to-all-start.5 = ((f32[1,2048,128]{2,0,1:T(1,128)}), f32[1,2048,128]{2,0,1:T(1,128)S(1)}, u32[]{:S(2)}, u32[]{:S(2)}) async-start(f32[1,2048,128]{2,0,1:T(1,128)} %bitcast.83), calls=%async_computation.5 | async-start | bytes 2097152 | tf_op jit(solution)/shard_map/all_to_all | solution.py:149
  198.2 4.5 %reshape.908 = s32[1,8,16,2048]{2,1,3,0:T(8,128)} reshape(s32[128,128,16]{0,2,1:T(8,128)S(1)} %broadcast_in_dim.21) | data formatting | bytes 2097152 | tf_op jit(solution)/shard_map/broadcast_in_dim | solution.py:167
  202.8 5.1 %copy.260 = s32[1,8,16,2048]{3,2,1,0:T(8,128)S(1)} copy(s32[1,8,16,2048]{2,1,3,0:T(8,128)} %reshape.908) | data formatting | bytes 2097152 | tf_op jit(solution)/shard_map/broadcast_in_dim | solution.py:167
  208.0 2.2 fusion.80
  210.2 2.2 fusion.66
  212.4 12.5 %all-to-all-done.5 = f32[1,2048,128]{2,0,1:T(1,128)S(1)} async-done(((f32[1,2048,128]{2,0,1:T(1,128)}), f32[1,2048,128]{2,0,1:T(1,128)S(1)}, u32[]{:S(2)}, u32[]{:S(2)}) %all-to-all-start.5) | async-done | bytes 1048608 | tf_op jit(solution)/shard_map/all_to_all | solution.py:149
  224.9 2.5 convolution_subtract_fusion.1
  227.4 1.4 multiply_add_fusion
  228.8 1.6 fusion.41
  230.4 2.4 multiply_reduce_fusion
  233.0 1.1 div.206
  234.1 31.9 %psum.14 = f32[1]{0:T(128)} all-reduce(f32[1]{0:T(128)} %bitcast.94), channel_id=1, replica_groups=mesh['maps'=2,'row'=4,'col'=4] {'row','col'}, use_global_device_ids=true, to_apply=%region_1.2 | all-reduce | flops 1 | bytes 8 | tf_op jit(solution)/shard_map/psum | solution.py:182
  266.8 1.1 broadcast_divide_fusion
  267.8 2.3 collective-permute-start
  271.9 2.0 collective-permute-done
  274.3 1.0 fusion.13
  275.3 3.2 %fusion.18 = f32[1,128,2048]{1,2,0:T(8,128)} fusion(f32[1,128,2048]{1,2,0:T(8,128)S(1)} %copy.231, f32[1,1,2048]{1,2,0:T(8,128)S(1)} %copy.230, f32[1,1,2048]{1,2,0:T(8,128)S(1)} %copy.223, f32[1,128,1]{1,2,0:T(1,128)S(1)} %get-tuple-element.19, f32[1,128,2047]{1,2,0:T(8,128)S(1)} %get-tuple-element.22, f32[1,128,1]{1,2,0:T(1,128)S(1)} %get-tuple-element.20, ...), kind=kLoop, calls=%fused_computation.51 | loop fusion | flops 5505024 | bytes 6383104 | tf_op jit(solution)/shard_map/jit(_where)/select_n | solution.py:178
  278.5 1.6 copy.232
  280.2 1.2 add_divide_fusion
  281.6 30.5 %psum.15 = f32[1,16]{1,0:T(1,128)} all-reduce(f32[1,16]{1,0:T(1,128)S(1)} %bitcast.269), channel_id=1, replica_groups=mesh['maps'=2,'row'=4,'col'=4] {'row','col'}, use_global_device_ids=true, to_apply=%region_5.6 | all-reduce | flops 16 | bytes 128 | tf_op jit(solution)/shard_map/psum | solution.py:191
  (41 shorter events, 4.4 us)
Async XLA Ops:
  4.4 32.1 %all-to-all-start.1 = ((f32[1,512,512]{2,0,1:T(1,128)}), f32[1,512,512]{2,0,1:T(1,128)S(1)}, u32[]{:S(2)}, u32[]{:S(2)}) async-start(f32[1,512,512]{2,0,1:T(1,128)} %bitcast.246), calls=%async_computation.1 | async-start | bytes 2097152 | tf_op jit(solution)/shard_map/all_to_all | solution.py:137
  36.5 28.9 %all-to-all-start = ((f32[1,512,512]{2,0,1:T(1,128)}), f32[1,512,512]{2,0,1:T(1,128)S(1)}, u32[]{:S(2)}, u32[]{:S(2)}) async-start(f32[1,512,512]{2,0,1:T(1,128)} %bitcast.247), calls=%async_computation | async-start | bytes 2097152 | tf_op jit(solution)/shard_map/all_to_all | solution.py:136
  76.2 31.0 %all-to-all-start.3 = ((f32[1,128,2048]{1,0,2:T(1,128)}), f32[1,128,2048]{1,0,2:T(1,128)S(1)}, u32[]{:S(2)}, u32[]{:S(2)}) async-start(f32[1,128,2048]{1,0,2:T(1,128)} %bitcast.32), calls=%async_computation.3 | async-start | bytes 2097152 | tf_op jit(solution)/shard_map/all_to_all | solution.py:142
  107.3 4.7 %copy-start.1 = (f32[1,128,2048]{1,0,2:T(1,128)}, f32[1,128,2048]{1,0,2:T(1,128)S(1)}, u32[]{:S(2)}) copy-start(f32[1,128,2048]{1,0,2:T(1,128)S(1)} %all-to-all-done.3) | copy-start | bytes 3145732
  107.3 30.5 %all-to-all-start.2 = ((f32[1,128,2048]{1,0,2:T(1,128)}), f32[1,128,2048]{1,0,2:T(1,128)S(1)}, u32[]{:S(2)}, u32[]{:S(2)}) async-start(f32[1,128,2048]{1,0,2:T(1,128)} %bitcast.25), calls=%async_computation.2 | async-start | bytes 2097152 | tf_op jit(solution)/shard_map/all_to_all | solution.py:141
  137.8 1.0 copy-start.2
  163.7 30.7 %all-to-all-start.4 = ((f32[1,2048,128]{2,0,1:T(1,128)}), f32[1,2048,128]{2,0,1:T(1,128)S(1)}, u32[]{:S(2)}, u32[]{:S(2)}) async-start(f32[1,2048,128]{2,0,1:T(1,128)} %bitcast.262), calls=%async_computation.4 | async-start | bytes 2097152 | tf_op jit(solution)/shard_map/all_to_all | solution.py:148
  170.8 27.2 %copy-start.4 = (s32[1,8,128]{2,1,0:T(8,128)S(1)}, s32[1,8,128]{2,1,0:T(8,128)}, u32[]{:S(2)}) copy-start(s32[1,8,128]{2,1,0:T(8,128)} %param.6) | copy-start | bytes 12292
  194.4 30.5 %all-to-all-start.5 = ((f32[1,2048,128]{2,0,1:T(1,128)}), f32[1,2048,128]{2,0,1:T(1,128)S(1)}, u32[]{:S(2)}, u32[]{:S(2)}) async-start(f32[1,2048,128]{2,0,1:T(1,128)} %bitcast.83), calls=%async_computation.5 | async-start | bytes 2097152 | tf_op jit(solution)/shard_map/all_to_all | solution.py:149
  202.8 5.2 %copy-start.5 = (s32[1,16]{1,0:T(1,128)S(1)}, s32[1,16]{1,0:T(1,128)}, u32[]{:S(2)}) copy-start(s32[1,16]{1,0:T(1,128)} %param.7) | copy-start | bytes 196
  224.9 2.6 copy-start
  234.1 36.0 %copy-start.3 = (f32[1,8,16,2048]{3,2,1,0:T(8,128)S(1)}, f32[1,8,16,2048]{3,2,1,0:T(8,128)}, u32[]{:S(2)}) copy-start(f32[1,8,16,2048]{3,2,1,0:T(8,128)} %div.206) | copy-start | bytes 3145732
  267.8 3.7 %collective-permute-start.1 = (f32[1,1,2048]{2,1,0:T(1,128)S(1)}, f32[1,1,2048]{2,1,0:T(1,128)S(1)}, u32[]{:S(2)}, u32[]{:S(2)}) collective-permute-start(f32[1,1,2048]{2,1,0:T(1,128)S(1)} %get-tuple-element.26), channel_id=1, source_target_pairs={{1,0},{2,1},{3,2},{4,3},{5,4},{6,5},{7,6},{8,7},{9,8},{10,9},{11,1... | collective-permute-start | bytes 24584 | tf_op jit(solution)/shard_map/ppermute | solution.py:29
  267.8 6.0 %collective-permute-start = (f32[1,1,2048]{2,1,0:T(1,128)S(1)}, f32[1,1,2048]{2,1,0:T(1,128)S(1)}, u32[]{:S(2)}, u32[]{:S(2)}) collective-permute-start(f32[1,1,2048]{2,1,0:T(1,128)S(1)} %get-tuple-element.25), channel_id=1, source_target_pairs={{0,1},{1,2},{2,3},{3,4},{4,5},{5,6},{6,7},{7,8},{8,9},{9,10},{10,1... | collective-permute-start | bytes 24584 | tf_op jit(solution)/shard_map/ppermute | solution.py:28
where the time goes:
time: 316 us; the launch traced here: 312 us
  waiting for transfers between devices  129 us (41%)
  blocking collectives  62.5 us (20%)
  matrix products  52.9 us (17%)
  local copies, waits for them, and re-layouts  31.3 us (10%)
  starting transfers between devices  27.7 us (9%)
  other arithmetic  6.31 us (2%)
    psum x1, blocking collectives, body(): total = lax.psum(jnp.sum(kappa * kappa, axis=(1, 2)), ('row', 'col'))  31.9 us
    psum x1, blocking collectives, body(): counts = lax.psum(local, ('row', 'col'))  30.5 us
    all_to_all x1, waiting for transfers between devices, spectral_pass(): lax.all_to_all(imag_part, 'col', split_axis=1, concat_axis=2, tiled=True)  23.7 us
    all_to_all x1, waiting for transfers between devices, spectral_pass(): lax.all_to_all(real_part, 'col', split_axis=1, concat_axis=2, tiled=True)  23 us
    all_to_all x1, waiting for transfers between devices, spectral_pass(): lax.all_to_all(real_part, ('row', 'col'), split_axis=2, concat_axis=1, ti...  23 us
    all_to_all x1, waiting for transfers between devices, spectral_pass(): lax.all_to_all(imag_part, ('row', 'col'), split_axis=2, concat_axis=1, ti...  22.7 us
    all_to_all x1, waiting for transfers between devices, spectral_pass(): lax.all_to_all(real_part, ('row', 'col'), split_axis=1, concat_axis=2, ti...  22.1 us
    dot_general x7, matrix products, cform(): apply(left[1], right[1])  13.6 us
  transfers between devices with their start and end apart: 8, of which 8 were waited for; matrix products, arithmetic and copies ran while one was open for 10% of the time, Pallas kernels for 0%

commit v1 on v0

v1 whole, which is shorter than its diff:
```python
from functools import partial
import math

import jax
import jax.numpy as jnp
import numpy as np
from jax import lax
from jax.experimental import pallas as pl
from jax.experimental.pallas import tpu as pltpu
from jax.sharding import PartitionSpec as P

LANES = 128
CELL = 16
MESH = pl.DeviceIdType.MESH
GROUP = ("row", "col")
PEAK_SOFT = 0.05
BIN_SOFT = 0.1
BIN_STEP = 0.25


def split_table(values):
    values = jnp.asarray(values.astype(np.float32))
    high = values.astype(jnp.bfloat16)
    low = (values - high.astype(jnp.float32)).astype(jnp.bfloat16)
    return high, low


def split_value(x):
    high = x.astype(jnp.bfloat16)
    return high, (x - high.astype(jnp.float32)).astype(jnp.bfloat16)


def mm(a, b):
    dot = partial(jnp.dot, preferred_element_type=jnp.float32)
    return dot(a[0], b[0]) + (dot(a[0], b[1]) + dot(a[1], b[0]))


def y_tables(length):
    radix = length // LANES
    half = LANES // 2
    i = np.arange(LANES)[:, None].astype(np.float64)
    l = np.arange(LANES)[None, :].astype(np.float64)
    th = 2 * np.pi * ((i * l) % LANES) / LANES
    c, s = np.cos(th), np.sin(th)

    def order(re, im):
        return np.concatenate([re[:, :half], im[:, :half], re[:, half:], im[:, half:]], axis=1)

    base = np.concatenate([order(c, -s), order(s, c)], axis=0)
    inv = np.concatenate([order(c, -s), order(s, c)], axis=0).T * 2.0 / length
    th0 = 2 * np.pi * ((i * l[:, :half]) % LANES) / LANES
    th8 = 2 * np.pi * ((i * (radix // 2 + radix * l[:, :half])) % length) / length
    zero = np.zeros_like(th0)
    im0 = -np.sin(th0)
    im0[:, 0] = (-1.0) ** np.arange(LANES)
    top = np.concatenate([np.cos(th0), im0, zero, zero], axis=1)
    bottom = np.concatenate([zero, zero, np.cos(th8), -np.sin(th8)], axis=1)
    first = np.concatenate([top, bottom], axis=0)
    first_inv = first.T * 2.0 / length
    first_inv[0] /= 2.0
    first_inv[half] /= 2.0
    k = np.arange(radix // 2)[:, None].astype(np.float64)
    tw = 2 * np.pi * k * np.arange(LANES)[None, :] / length
    return base, first, inv, first_inv, np.cos(tw), np.sin(tw)


def x_tables(length):
    radix = length // LANES
    i = np.arange(LANES)[:, None].astype(np.float64)
    th = 2 * np.pi * ((i * i.T) % LANES) / LANES
    fwd = np.concatenate([np.cos(th), -np.sin(th)], axis=1)
    inv = np.concatenate([np.cos(th), np.sin(th)], axis=1) / length
    tw = 2 * np.pi * i * np.arange(radix)[None, :] / length
    return fwd, inv, np.concatenate([np.cos(tw), np.sin(tw)], axis=1)


def cs(k, n, radix):
    a = (k * n) % radix
    c, s = math.cos(2 * math.pi * a / radix), math.sin(2 * math.pi * a / radix)
    return round(c, 15), round(s, 15)


def axpy(total, coef, x):
    if coef == 0.0:
        return total
    if coef == 1.0:
        return x if total is None else total + x
    if coef == -1.0:
        return -x if total is None else total - x
    return coef * x if total is None else total + coef * x


def cos_sin_sums(parts):
    radix = len(parts)
    h = radix // 2
    plus = [None] + [parts[n] + parts[radix - n] for n in range(1, h)]
    minus = [None] + [parts[n] - parts[radix - n] for n in range(1, h)]
    pe, po = parts[0] + parts[h], parts[0] - parts[h]
    out = []
    for k in range(h // 2 + 1):
        ce = pe if k % 2 == 0 else po
        co = None
        se = so = None
        for n in range(1, h):
            c, s = cs(k, n, radix)
            if n % 2 == 0:
                ce = axpy(ce, c, plus[n])
                se = axpy(se, s, minus[n])
            else:
                co = axpy(co, c, plus[n])
                so = axpy(so, s, minus[n])
        out.append((ce, co, se, so))
    res = [None] * (h + 1)

    def add(a, b, sign):
        if a is None:
            return None if b is None else (b if sign > 0 else -b)
        if b is None:
            return a
        return a + b if sign > 0 else a - b

    for k in range(h // 2 + 1):
        ce, co, se, so = out[k]
        res[k] = (add(ce, co, 1), add(se, so, 1))
        if k != h - k:
            res[h - k] = (add(ce, co, -1), add(so, se, -1))
    return res


def forward_y_kernel(x_ref, bh, bl, fh, fl, tc, ts, out_ref):
    cols, rows, width = x_ref.shape[1:]
    per = width // LANES
    step = 32
    base, first = (bh[...], bl[...]), (fh[...], fl[...])
    for f in range(2):
        stage = []
        blocks = [x_ref[f, c, :, m * LANES : (m + 1) * LANES] for c in range(cols) for m in range(per)]
        sums = cos_sin_sums(blocks)
        h = len(blocks) // 2
        for k in range(h):
            if k == 0:
                both = jnp.concatenate([sums[0][0], sums[h][0]], axis=1)
                table = first
            else:
                re, im = sums[k][0], -sums[k][1]
                c, s = tc[k : k + 1, :], ts[k : k + 1, :]
                both = jnp.concatenate([re * c + im * s, im * c - re * s], axis=1)
                table = base
            got = mm(split_value(both), table)
            out_ref[2 * k, f] = got[:, :LANES]
            out_ref[2 * k + 1, f] = got[:, LANES:]


def turn(x, sign):
    return pltpu.roll(x, LANES // 2, 1) * sign


def middle_kernel(rows_total, x_ref, smooth_ref, fh, fl, ih, il, tw_ref, out_ref):
    length = rows_total
    radix = length // LANES
    h = radix // 2
    half = LANES // 2
    me = lax.axis_index("row") * lax.axis_size("col") + lax.axis_index("col")
    lane = lax.broadcasted_iota(jnp.int32, (LANES, LANES), 1)
    row = lax.broadcasted_iota(jnp.int32, (LANES, LANES), 0)
    sign = jnp.where(lane < half, -1.0, 1.0)
    slot = me * half + lane % half
    block, spot = slot // LANES, slot % LANES
    freq = jnp.where(
        block == 0,
        jnp.where(spot < half, radix * spot, h + radix * (spot - half)),
        block + radix * spot,
    )
    packed = slot == 0
    ky = jnp.where(freq < length // 2, freq, freq - length).astype(jnp.float32)
    one = [x_ref[n, 0] for n in range(radix)]
    two_raw = [x_ref[n, 1] for n in range(radix)]
    alternate = jnp.where(row % 2 == 0, 1.0, -1.0)
    total = two_raw[0]
    for n in range(1, radix):
        total = total + two_raw[n]
    corner = jnp.sum(total * alternate, axis=0, keepdims=True)
    two = [jnp.where(packed, -sign * a, b) for a, b in zip(one, two_raw)]
    sums = (cos_sin_sums(one), cos_sin_sums(two))
    fwd, inv = (fh[...], fl[...]), (ih[...], il[...])
    width = smooth_ref[0]
    scale = -2.0 * math.pi**2 * width * width
    edge = -float(length // 2)
    results = []
    for k in range(radix):
        j = min(k, radix - k)
        wc, ws = tw_ref[:, k : k + 1], tw_ref[:, radix + k : radix + k + 1]
        cols = []
        for f in range(2):
            c, s = sums[f][j]
            x = c
            if s is not None:
                x = c - turn(s, sign) if k == j else c + turn(s, sign)
            ix = turn(x, sign)
            if k:
                x, ix = wc * x - ws * ix, wc * ix + ws * x
            cols.append(jnp.concatenate([x, ix], axis=0))
        got = mm(fwd, split_value(jnp.concatenate(cols, axis=1)))
        g1, g2 = got[:, :LANES], got[:, LANES:]
        fx = k + radix * row
        kx = jnp.where(fx < length // 2, fx, fx - length).astype(jnp.float32)

        def kernel(ky):
            square = jnp.maximum(kx * kx + ky * ky, 1.0)
            damp = jnp.exp(scale * ((kx / length) ** 2 + (ky / length) ** 2))
            inverse = damp / square
            return (kx * kx - ky * ky) * inverse, -2.0 * kx * ky * inverse, damp

        kr, ki, _ = kernel(ky)
        nr, ni, damp_n = kernel(edge)
        last = fx == length // 2
        nr = jnp.where(last, 0.0, nr)
        ni_in = jnp.where(last, 0.0, ni)
        w1r = jnp.where(packed, 0.5 * (kr + nr), kr)
        w1i = jnp.where(packed, 0.5 * ni_in, jnp.where(last, ki, 0.0))
        w2r = jnp.where(packed, 0.5 * (kr - nr), jnp.where(last, 0.0, -ki))
        w2i = jnp.where(packed, -0.5 * ni_in, 0.0)
        z = w1r * g1 + w1i * turn(g1, sign) + w2r * g2 + w2i * turn(g2, sign)
        if k == 0:
            extra = jnp.where(packed & last & (lane >= half), -ni * corner, 0.0)
            z = z + extra
        iz = turn(z, sign)
        t = mm(inv, split_value(jnp.concatenate([z, iz], axis=0)))
        if k:
            t = wc * t + ws * turn(t, sign)
        results.append(t)
    sums = cos_sin_sums(results)
    for n in range(radix):
        j = min(n, radix - n)
        c, s = sums[j]
        x = c
        if s is not None:
            x = c + turn(s, sign) if n == j else c - turn(s, sign)
        out_ref[n] = x


def inverse_y_kernel(z_ref, bh, bl, fh, fl, tc, ts, out_ref, sq_ref, top_ref, bot_ref):
    count, rows, _ = z_ref.shape
    h = count // 2
    radix = count
    base, first = (bh[...], bl[...]), (fh[...], fl[...])
    real, imag = [None] * (h + 1), [None] * (h + 1)
    for k in range(h):
        both = jnp.concatenate([z_ref[2 * k], z_ref[2 * k + 1]], axis=1)
        got = mm(split_value(both), first if k == 0 else base)
        a, b = got[:, :LANES], got[:, LANES:]
        if k == 0:
            real[0], real[h] = a, b
        else:
            c, s = tc[k : k + 1, :], ts[k : k + 1, :]
            real[k], imag[k] = a * c - b * s, a * s + b * c
    square = None
    for n in range(h + 1):
        cosine, sine = real[0], None
        cosine = cosine + real[h] if n % 2 == 0 else cosine - real[h]
        for k in range(1, h):
            c, s = cs(k, n, radix)
            cosine = axpy(cosine, c, real[k])
            sine = axpy(sine, s, imag[k])
        for m in {n, (radix - n) % radix}:
            if sine is None:
                out = cosine
            else:
                out = cosine - sine if m == n else cosine + sine
            sl = slice(m * LANES, (m + 1) * LANES)
            out_ref[:, sl] = out
            top_ref[:, sl] = out[:1]
            bot_ref[:, sl] = out[rows - 1 :]
            sq = out * out
            square = sq if square is None else square + sq
    sq_ref[...] = jnp.sum(square, axis=0, keepdims=True)


def place():
    cols = lax.axis_size("col")
    count = lax.axis_size("row") * cols
    me = lax.axis_index("row") * cols + lax.axis_index("col")

    def at(d):
        peer = lax.rem(me + d, count)
        return {"row": peer // cols, "col": lax.rem(peer, cols)}

    return count, me, at


def greet(count, at):
    barrier = pltpu.get_barrier_semaphore()
    for d in range(1, count):
        pl.semaphore_signal(barrier, inc=1, device_id=at(d), device_id_type=MESH)
    pl.semaphore_wait(barrier, count - 1)


def spread(count, at, src, slots, send, recv):
    copies = []
    for d in range(1, count):
        copy = pltpu.make_async_remote_copy(
            src_ref=src, dst_ref=slots.at[d - 1], send_sem=send.at[d - 1],
            recv_sem=recv.at[d - 1], device_id=at(d), device_id_type=MESH,
        )
        copy.start()
        copies.append(copy)
    return copies


def sum_kernel(x_ref, out_ref, slots, send, recv):
    count, _, at = place()
    greet(count, at)
    for copy in spread(count, at, x_ref, slots, send, recv):
        copy.wait()
    total = x_ref[...]
    for d in range(1, count):
        total = total + slots[d - 1]
    out_ref[...] = total


def edge_kernel(sq_ref, top_ref, bot_ref, out_ref, above_ref, below_ref, slots, send, recv, hsend, hrecv):
    count, _, at = place()
    greet(count, at)
    copies = spread(count, at, sq_ref, slots, send, recv)
    for i, (src, dst, d) in enumerate(((bot_ref, above_ref, 1), (top_ref, below_ref, count - 1))):
        copy = pltpu.make_async_remote_copy(
            src_ref=src, dst_ref=dst, send_sem=hsend.at[i], recv_sem=hrecv.at[i],
            device_id=at(d), device_id_type=MESH,
        )
        copy.start()
        copies.append(copy)
    for copy in copies:
        copy.wait()
    total = sq_ref[...]
    for d in range(1, count):
        total = total + slots[d - 1]
    out_ref[...] = total


def peak_kernel(pixels, x_ref, above_ref, below_ref, sq_ref, off_ref, thr_ref, snr_ref, high_ref, cnt_ref, wide):
    rows, width = x_ref.shape
    cells = width // CELL
    pad = 8
    rms = jnp.sqrt(jnp.sum(sq_ref[...], axis=1, keepdims=True) / pixels + 1e-06)

    def three(x):
        side = jnp.maximum(pltpu.roll(x, 1, 1), pltpu.roll(x, width - 1, 1))
        return side, jnp.maximum(side, x)

    wide[pad - 1 : pad, :] = three(jnp.broadcast_to(above_ref[...], (8, width)))[1][:1]
    wide[pad + rows : pad + rows + 1, :] = three(jnp.broadcast_to(below_ref[...], (8, width)))[1][:1]
    for p in range(rows // CELL):
        sl = slice(p * CELL, (p + 1) * CELL)
        wide[pad + p * CELL : pad + (p + 1) * CELL, :] = three(x_ref[sl, :])[1]
    same = lax.broadcasted_iota(jnp.int32, (cells, width), 1) // CELL == lax.broadcasted_iota(
        jnp.int32, (cells, width), 0
    )
    spread_table = same.astype(jnp.bfloat16)
    full = jnp.dot(
        off_ref[...].astype(jnp.bfloat16), spread_table, preferred_element_type=jnp.float32
    ).astype(jnp.int32)
    code = lax.broadcasted_iota(jnp.int32, (CELL, width), 0) * CELL + (
        lax.broadcasted_iota(jnp.int32, (CELL, width), 1) % CELL
    )
    tops, mids = [], []
    for p in range(rows // CELL):
        low = pad + p * CELL
        x = x_ref[p * CELL : (p + 1) * CELL, :]
        snr_ref[p * CELL : (p + 1) * CELL, :] = x / rms
        near = jnp.maximum(
            three(x)[0],
            jnp.maximum(wide[low - 1 : low - 1 + CELL, :], wide[low + 1 : low + 1 + CELL, :]),
        )
        chosen = full[p : p + 1, :] == code
        tops.append(jnp.sum(jnp.where(chosen, x - near, 0.0), axis=0, keepdims=True))
        mids.append(jnp.sum(jnp.where(chosen, x, 0.0), axis=0, keepdims=True))

    def gather(parts):
        dot = partial(
            lax.dot_general, dimension_numbers=(((1,), (1,)), ((), ())),
            preferred_element_type=jnp.float32,
        )
        x = jnp.concatenate(parts, axis=0)
        a = x.astype(jnp.bfloat16)
        rest = x - a.astype(jnp.float32)
        b = rest.astype(jnp.bfloat16)
        c = (rest - b.astype(jnp.float32)).astype(jnp.bfloat16)
        return dot(a, spread_table) + (dot(b, spread_table) + dot(c, spread_table))

    heights = gather(tops) / rms
    values = gather(mids) / rms
    high_ref[...] = heights
    weight = 1.0 / (1.0 + jnp.exp(-heights / PEAK_SOFT))
    lane = lax.broadcasted_iota(jnp.int32, (1, LANES), 1)
    counts = jnp.zeros((1, LANES), jnp.float32)
    for k in range(thr_ref.shape[0]):
        level = BIN_STEP * thr_ref[k].astype(jnp.float32)
        above = weight / (1.0 + jnp.exp((level - values) / BIN_SOFT))
        one = jnp.sum(jnp.sum(above, axis=0, keepdims=True), axis=1, keepdims=True)
        counts = jnp.where(lane == k, one, counts)
    cnt_ref[...] = counts


VM = pl.BlockSpec(memory_space=pltpu.VMEM)
SM = pl.BlockSpec(memory_space=pltpu.SMEM)
F32 = jnp.float32


def shape(*dims):
    return jax.ShapeDtypeStruct(dims, F32)


def call(kernel, out_shape, specs, scratch=(), **params):
    outs = out_shape if isinstance(out_shape, tuple) else None
    return pl.pallas_call(
        kernel,
        out_shape=out_shape,
        in_specs=specs,
        out_specs=VM if outs is None else tuple(VM for _ in outs),
        scratch_shapes=list(scratch),
        compiler_params=pltpu.CompilerParams(vmem_limit_bytes=40 * 2**20, **params),
    )


def one_map(shear, smoothing, offsets, thresholds):
    rows_in, cols_in = shear.shape[1:]
    nrow, ncol = lax.axis_size("row"), lax.axis_size("col")
    nx, ny = rows_in * nrow, cols_in * ncol
    count = nrow * ncol
    rows = nx // count
    base, first, inv, first_inv, tc, ts = y_tables(ny)
    fwd_x, inv_x, tw_x = x_tables(nx)
    tc, ts, tw_x = (jnp.asarray(t.astype(np.float32)) for t in (tc, ts, tw_x))
    x = shear.reshape(2, ncol, rows, cols_in)
    x = lax.all_to_all(x, "col", split_axis=1, concat_axis=1, tiled=True)
    x = call(forward_y_kernel, shape(count, 2, rows, LANES), [VM] * 7)(
        x, *split_table(base), *split_table(first), tc, ts
    )
    x = lax.all_to_all(x, GROUP, split_axis=0, concat_axis=0, tiled=True)
    x = call(partial(middle_kernel, nx), shape(count, rows, LANES), [VM, SM] + [VM] * 5)(
        x, smoothing, *split_table(fwd_x), *split_table(inv_x), tw_x
    )
    x = lax.all_to_all(x, GROUP, split_axis=0, concat_axis=0, tiled=True)
    kappa, sq, top, bot = call(
        inverse_y_kernel,
        (shape(rows, ny), shape(1, LANES), shape(1, ny), shape(1, ny)),
        [VM] * 7,
    )(x, *split_table(inv), *split_table(first_inv), tc, ts)
    dma = pltpu.SemaphoreType.DMA
    slots = [pltpu.VMEM((count - 1, 1, LANES), F32), dma((count - 1,)), dma((count - 1,))]
    sq, above, below = call(
        edge_kernel,
        (shape(1, LANES), shape(1, ny), shape(1, ny)),
        [VM] * 3,
        slots + [dma((2,)), dma((2,))],
        collective_id=0,
        has_side_effects=True,
    )(sq, top, bot)
    snr, heights, local = call(
        partial(peak_kernel, float(nx * ny)),
        (shape(rows, ny), shape(*offsets.shape), shape(1, LANES)),
        [VM] * 5 + [SM],
        [pltpu.VMEM((rows + 16, ny), F32)],
    )(kappa, above, below, sq, offsets, thresholds)
    counts = call(
        sum_kernel, shape(1, LANES), [VM], slots, collective_id=1, has_side_effects=True
    )(local)
    return snr, heights, counts[0, : thresholds.shape[0]]


def body(shear, smoothing, offsets, thresholds):
    outs = [
        one_map(shear[:, m], smoothing[m : m + 1], offsets[m], thresholds[m])
        for m in range(shear.shape[1])
    ]
    return tuple(jnp.stack(parts) for parts in zip(*outs))


def solution(mesh):
    return jax.shard_map(
        body,
        mesh=mesh,
        in_specs=(
            P(None, "maps", "row", "col"),
            P("maps"),
            P("maps", GROUP, None),
            P("maps", None),
        ),
        out_specs=(P("maps", GROUP, None), P("maps", GROUP, None), P("maps", None)),
        check_vma=False,
    )
```

time: 316 us -> 169 us (0.53)
  waiting for transfers between devices: 129 us -> 48.6 us
  matrix products: 52.9 us -> 0 us
  local copies, waits for them, and re-layouts: 31.3 us -> 4.79 us
  Pallas kernels: 0 us -> 24.9 us
  starting transfers between devices: 27.7 us -> 4.08 us
  blocking collectives: 62.5 us -> 84.4 us
  other arithmetic: 6.31 us -> 0 us
    all_to_all x0 -> x2, blocking collectives: none -> 84.4 us  [the longest x1 54.3 us: one_map(): x = lax.all_to_all(x, 'col', split_axis=1, concat_axis=1, tiled=True)]
    all_to_all x6 -> x1, waiting for transfers between devices: 127 us -> 48.6 us  [one_map(): x = lax.all_to_all(x, GROUP, split_axis=0, concat_axis=0, tiled=True)]
    psum x2 -> x0, blocking collectives: 62.5 us -> none  [the longest x1 31.9 us: body(): total = lax.psum(jnp.sum(kappa * kappa, axis=(1, 2)), ('row', 'col'))]
    dot_general x32 -> x0, matrix products: 52.9 us -> none  [the longest x7 13.6 us: cform(): apply(left[1], right[1])]
    pallas_call x0 -> x6, Pallas kernels: none -> 24.9 us  [the longest x1 6.86 us: one_map(): call(edge_kernel, (shape(1, LANES), shape(1, ny), shape(1, ny)), [VM] * 3...]
    all_to_all x6 -> x1, starting transfers between devices: 25.4 us -> 4.08 us  [one_map(): x = lax.all_to_all(x, GROUP, split_axis=0, concat_axis=0, tiled=True)]
    broadcast_in_dim x5 -> x0, local copies, waits for them, and re-layouts: 9.82 us -> none  [body(): full = jnp.repeat(jnp.repeat(offsets, CELL, axis=1), CELL, axis=2)]
    all_to_all x4 -> x1, local copies, waits for them, and re-layouts: 5.78 us -> 0.17 us  [one_map(): x = lax.all_to_all(x, 'col', split_axis=1, concat_axis=1, tiled=True)]
  transfers between devices with their start and end apart: 8 -> 1, of which waited for: 8 -> 1; matrix products, arithmetic and copies ran while one was open for 10% -> 0% of each run, Pallas kernels for 0% -> 0%
where the time goes in v1:
time: 169 us; the launch traced here: 168 us
  blocking collectives  84.4 us (50%)
  waiting for transfers between devices  48.6 us (29%)
  Pallas kernels  24.9 us (15%)
  local copies, waits for them, and re-layouts  4.79 us (3%)
  starting transfers between devices  4.08 us (2%)
    all_to_all x1, blocking collectives, one_map(): x = lax.all_to_all(x, 'col', split_axis=1, concat_axis=1, tiled=True)  54.3 us
    all_to_all x1, waiting for transfers between devices, one_map(): x = lax.all_to_all(x, GROUP, split_axis=0, concat_axis=0, tiled=True)  48.6 us
    all_to_all x1, blocking collectives, one_map(): x = lax.all_to_all(x, GROUP, split_axis=0, concat_axis=0, tiled=True)  30.1 us
    pallas_call x1, Pallas kernels, one_map(): call(edge_kernel, (shape(1, LANES), shape(1, ny), shape(1, ny)), [VM] * 3...  6.86 us
    pallas_call x1, Pallas kernels, one_map(): call(sum_kernel, shape(1, LANES), [VM], slots, collective_id=1, has_side_...  6.6 us
    pallas_call x1, Pallas kernels, one_map(): call(partial(middle_kernel, nx), shape(count, rows, LANES), [VM, SM] + [V...  5.66 us
    all_to_all x1, starting transfers between devices, one_map(): x = lax.all_to_all(x, GROUP, split_axis=0, concat_axis=0, tiled=True)  4.08 us
    pallas_call x1, Pallas kernels, one_map(): call(partial(peak_kernel, float(nx * ny)), (shape(rows, ny), shape(*offse...  3.54 us
  transfers between devices with their start and end apart: 1, of which 1 were waited for; matrix products, arithmetic and copies ran while one was open for 0% of the time, Pallas kernels for 0%

profile of v1, /device:TPU:0, one launch (start us, length us, event | category | flops | bytes accessed | tf_op | source)
XLA Modules:
  0.0 168.3 jit_solution(8475787467380922894)
XLA Ops:
  0.6 1.8 %copy.17 = f32[2,4,128,512]{3,2,0,1:T(8,128)S(1)} copy(f32[2,4,128,512]{3,2,1,0:T(8,128)} %bitcast.9) | data formatting | bytes 4194304 | tf_op jit(solution)/shard_map/reshape;squeeze | solution.py:434
  2.5 54.3 %all_to_all.15 = f32[2,4,128,512]{3,2,0,1:T(8,128)S(1)} all-to-all(f32[2,4,128,512]{3,2,0,1:T(8,128)S(1)} %copy.17), channel_id=1, replica_groups=mesh['maps'=2,'row'=4,'col'=4] {'col'}, dimensions={1} | all-to-all | bytes 4194304 | tf_op jit(solution)/shard_map/all_to_all | solution.py:435
  56.8 0.0 copy-start.5
  56.8 0.0 copy-start.6
  56.8 0.0 copy-start.7
  56.8 0.0 copy-start.8
  56.8 0.0 copy-start.14
  56.8 0.0 copy-start.15
  56.8 0.2 copy.18.x_ref
  57.0 0.7 copy-done.5
  57.7 0.1 copy-done.6
  57.8 0.1 copy-done.7
  57.8 0.1 copy-done.8
  57.9 0.0 copy-done.14
  57.9 0.0 copy-done.15
  57.9 1.3 shard_map.148
  59.2 0.0 copy-start
  59.2 1.3 copy-done
  60.6 0.0 copy-start.9
  60.6 0.0 copy-start.10
  60.6 0.0 copy-start.11
  60.6 0.0 copy-start.12
  60.6 0.0 copy-start.13
  60.6 4.1 %all-to-all-start.1 = ((f32[16,2,128,128]{3,2,1,0:T(8,128)}), f32[16,2,128,128]{3,2,1,0:T(8,128)S(1)}, u32[]{:S(2)}, u32[]{:S(2)}) async-start(f32[16,2,128,128]{3,2,1,0:T(8,128)} %copy-done), calls=%async_computation.1 | async-start | bytes 4194304 | tf_op jit(solution)/shard_map/all_to_all | solution.py:439
  65.3 0.0 copy-start.1
  65.3 0.0 copy-start.2
  65.3 0.0 copy-start.3
  65.4 0.0 copy-start.4
  65.4 48.6 %all-to-all-done.1.x_ref = f32[16,2,128,128]{3,2,1,0:T(8,128)S(1)} async-done(((f32[16,2,128,128]{3,2,1,0:T(8,128)}), f32[16,2,128,128]{3,2,1,0:T(8,128)S(1)}, u32[]{:S(2)}, u32[]{:S(2)}) %all-to-all-start.1) | async-done | bytes 2097184 | tf_op jit(solution)/shard_map/all_to_all | solution.py:439
  114.0 0.0 copy-done.9
  114.0 0.0 copy-done.10
  114.0 0.0 copy-done.11
  114.0 0.0 copy-done.12
  114.0 0.0 copy-done.13
  114.0 5.7 %shard_map.149 = f32[16,128,128]{2,1,0:T(8,128)S(1)} custom-call(f32[16,2,128,128]{3,2,1,0:T(8,128)S(1)} %all-to-all-done.1.x_ref, f32[1]{0:T(128)S(6)} %copy.20.smooth_ref, bf16[128,256]{1,0:T(8,128)(2,1)S(1)} %copy-done.10, bf16[128,256]{1,0:T(8,128)(2,1)S(1)} %copy-done.11, bf16[128,256]{1,0:T(8,128)(2,1)S(1)} %copy-done.12, ...), custom_call_target="tpu_custom_call" | custom-call | tf_op jit(solution)/shard_map/pallas_call | solution.py:440
  119.7 0.0 copy-start.16
  119.7 0.0 copy-start.17
  119.7 30.1 %all_to_all.16.z_ref = f32[16,128,128]{2,1,0:T(8,128)S(1)} all-to-all(f32[16,128,128]{2,1,0:T(8,128)S(1)} %shard_map.149), channel_id=1, replica_groups=mesh['maps'=2,'row'=4,'col'=4] {'row','col'}, dimensions={0} | all-to-all | bytes 2097152 | tf_op jit(solution)/shard_map/all_to_all | solution.py:443
  149.8 0.0 copy-done.1
  149.8 0.0 copy-done.2
  149.8 0.0 copy-done.3
  149.8 0.0 copy-done.4
  149.8 0.9 shard_map.150
  150.7 6.9 %shard_map.151 = (f32[1,128]{1,0:T(1,128)S(1)}, f32[1,2048]{1,0:T(1,128)S(1)}, f32[1,2048]{1,0:T(1,128)S(1)}) custom-call(f32[1,128]{1,0:T(1,128)S(1)} %get-tuple-element.14.sq_ref, f32[1,2048]{1,0:T(1,128)S(1)} %get-tuple-element.15.top_ref, f32[1,2048]{1,0:T(1,128)S(1)} %get-tuple-element.16.bot_ref), custom_call_target="tpu_custom_call" | custom-call | tf_op jit(solution)/shard_map/pallas_call | solution.py:451
  157.6 0.0 copy-done.16
  157.6 0.0 copy-done.17
  157.6 3.5 %shard_map.152 = (f32[128,2048]{1,0:T(8,128)}, f32[8,128]{1,0:T(8,128)}, f32[1,128]{1,0:T(1,128)S(1)}) custom-call(f32[128,2048]{1,0:T(8,128)S(1)} %get-tuple-element.13.x_ref, f32[1,2048]{1,0:T(1,128)S(1)} %get-tuple-element.17.above_ref, f32[1,2048]{1,0:T(1,128)S(1)} %get-tuple-element.18.below_ref, f32[1,128]{1,0:T(1,128)S(1)} %get-tuple-element.19.sq_ref, ...), custom_call_target="tpu_custom_call" | custom-call | tf_op jit(solution)/shard_map/pallas_call | solution.py:459
  161.1 6.6 %shard_map.153 = f32[1,128]{1,0:T(1,128)S(1)} custom-call(f32[1,128]{1,0:T(1,128)S(1)} %get-tuple-element.22.x_ref), custom_call_target="tpu_custom_call" | custom-call | tf_op jit(solution)/shard_map/pallas_call | solution.py:465
  167.7 0.5 copy.21
Async XLA Ops:
  56.8 0.9 copy-start.5
  56.8 1.0 copy-start.6
  56.8 1.0 copy-start.7
  56.8 1.1 copy-start.8
  56.8 1.1 copy-start.14
  56.8 1.1 copy-start.15
  59.2 1.3 copy-start
  60.6 53.4 %copy-start.9 = (f32[128,32]{1,0:T(8,128)S(1)}, f32[128,32]{1,0:T(8,128)}, u32[]{:S(2)}) copy-start(f32[128,32]{1,0:T(8,128)} %constant.20.clone.tw_ref) | copy-start | bytes 49156
  60.6 53.4 %copy-start.10 = (bf16[128,256]{1,0:T(8,128)(2,1)S(1)}, bf16[128,256]{1,0:T(8,128)(2,1)}, u32[]{:S(2)}) copy-start(bf16[128,256]{1,0:T(8,128)(2,1)} %constant.39.fh) | copy-start | bytes 196612
  60.6 53.4 %copy-start.11 = (bf16[128,256]{1,0:T(8,128)(2,1)S(1)}, bf16[128,256]{1,0:T(8,128)(2,1)}, u32[]{:S(2)}) copy-start(bf16[128,256]{1,0:T(8,128)(2,1)} %constant.42.fl) | copy-start | bytes 196612
  60.6 53.4 %copy-start.12 = (bf16[128,256]{1,0:T(8,128)(2,1)S(1)}, bf16[128,256]{1,0:T(8,128)(2,1)}, u32[]{:S(2)}) copy-start(bf16[128,256]{1,0:T(8,128)(2,1)} %constant.43.ih) | copy-start | bytes 196612
  60.6 53.4 %copy-start.13 = (bf16[128,256]{1,0:T(8,128)(2,1)S(1)}, bf16[128,256]{1,0:T(8,128)(2,1)}, u32[]{:S(2)}) copy-start(bf16[128,256]{1,0:T(8,128)(2,1)} %constant.46.il) | copy-start | bytes 196612
  60.6 53.4 %all-to-all-start.1 = ((f32[16,2,128,128]{3,2,1,0:T(8,128)}), f32[16,2,128,128]{3,2,1,0:T(8,128)S(1)}, u32[]{:S(2)}, u32[]{:S(2)}) async-start(f32[16,2,128,128]{3,2,1,0:T(8,128)} %copy-done), calls=%async_computation.1 | async-start | bytes 4194304 | tf_op jit(solution)/shard_map/all_to_all | solution.py:439
  65.3 84.4 %copy-start.1 = (bf16[256,256]{1,0:T(8,128)(2,1)S(1)}, bf16[256,256]{1,0:T(8,128)(2,1)}, u32[]{:S(2)}) copy-start(bf16[256,256]{1,0:T(8,128)(2,1)} %constant.47.bh) | copy-start | bytes 393220
  65.3 84.4 %copy-start.2 = (bf16[256,256]{1,0:T(8,128)(2,1)S(1)}, bf16[256,256]{1,0:T(8,128)(2,1)}, u32[]{:S(2)}) copy-start(bf16[256,256]{1,0:T(8,128)(2,1)} %constant.50.bl) | copy-start | bytes 393220
  65.3 84.4 %copy-start.3 = (bf16[256,256]{1,0:T(8,128)(2,1)S(1)}, bf16[256,256]{1,0:T(8,128)(2,1)}, u32[]{:S(2)}) copy-start(bf16[256,256]{1,0:T(8,128)(2,1)} %constant.51.fh) | copy-start | bytes 393220
  65.4 84.4 %copy-start.4 = (bf16[256,256]{1,0:T(8,128)(2,1)S(1)}, bf16[256,256]{1,0:T(8,128)(2,1)}, u32[]{:S(2)}) copy-start(bf16[256,256]{1,0:T(8,128)(2,1)} %constant.54.fl) | copy-start | bytes 393220
  119.7 37.9 %copy-start.16 = (s32[1,8,128]{2,1,0:T(8,128)S(1)}, s32[1,8,128]{2,1,0:T(8,128)}, u32[]{:S(2)}) copy-start(s32[1,8,128]{2,1,0:T(8,128)} %param.15) | copy-start | bytes 12292
  119.7 37.9 %copy-start.17 = (s32[1,16]{1,0:T(1,128)S(1)}, s32[1,16]{1,0:T(1,128)}, u32[]{:S(2)}) copy-start(s32[1,16]{1,0:T(1,128)} %param.16) | copy-start | bytes 196

commit v2 on v1

--- a/solution.py
+++ b/solution.py
@@ -127,14 +127,70 @@
     return res
 
 
-def forward_y_kernel(x_ref, bh, bl, fh, fl, tc, ts, out_ref):
-    cols, rows, width = x_ref.shape[1:]
+def masked(index, size, m):
+    assert size == 4
+    return (index, index + 1 - 2 * lax.rem(index, 2), lax.rem(index + 2, 4), 3 - index)[m]
+
+
+def partners():
+    nrow, ncol = lax.axis_size("row"), lax.axis_size("col")
+    far = list(range(ncol // 2, ncol)) + list(range(ncol // 2))
+    return [(p, q) for q in far for p in reversed(range(nrow))]
+
+
+def seat(p, q):
+    row = masked(lax.axis_index("row"), lax.axis_size("row"), p)
+    col = masked(lax.axis_index("col"), lax.axis_size("col"), q)
+    return row, col, row * lax.axis_size("col") + col
+
+
+def deal(src_of, dst, send, recv, local):
+    _, me, _ = place()
+    copies = []
+    own = pltpu.make_async_copy(src_of(me), dst, local)
+    own.start()
+    for i, (p, q) in enumerate(partners()):
+        row, col, peer = seat(p, q)
+        if p == 0 and q == 0:
+            continue
+        copy = pltpu.make_async_remote_copy(
+            src_ref=src_of(peer), dst_ref=dst, send_sem=send.at[i], recv_sem=recv.at[i],
+            device_id={"row": row, "col": col}, device_id_type=MESH,
+        )
+        copy.start()
+        copies.append(copy)
+    return copies + [own]
+
+
+def forward_y_kernel(shear, bh, bl, fh, fl, tc, ts, out_ref, xbuf, sbuf, asend, arecv, bsend, brecv, loc):
+    _, cols, rows, width = xbuf.shape
     per = width // LANES
-    step = 32
+    count, me, at = place()
+    greet(count, at)
+    here = lax.axis_index("col")
+    arrive = []
+    for f in range(2):
+        copies = []
+        for q in list(range(cols // 2, cols)) + list(range(cols // 2)):
+            other = masked(here, cols, q)
+            src = shear.at[f, pl.ds(pl.multiple_of(other * rows, rows), rows), :]
+            dst = xbuf.at[f, here]
+            if q == 0:
+                copy = pltpu.make_async_copy(src, dst, loc.at[f])
+            else:
+                copy = pltpu.make_async_remote_copy(
+                    src_ref=src, dst_ref=dst, send_sem=asend.at[f, q], recv_sem=arecv.at[f, q],
+                    device_id={"col": other}, device_id_type=MESH,
+                )
+            copy.start()
+            copies.append(copy)
+        arrive.append(copies)
     base, first = (bh[...], bl[...]), (fh[...], fl[...])
+    leave = []
     for f in range(2):
-        stage = []
-        blocks = [x_ref[f, c, :, m * LANES : (m + 1) * LANES] for c in range(cols) for m in range(per)]
+        for copy in arrive[f]:
+            copy.wait()
+        blocks = [xbuf[f, c, :, m * LANES : (m + 1) * LANES] for c in range(cols) for m in range(per)]
         sums = cos_sin_sums(blocks)
         h = len(blocks) // 2
         for k in range(h):
@@ -147,20 +203,26 @@
                 both = jnp.concatenate([re * c + im * s, im * c - re * s], axis=1)
                 table = base
             got = mm(split_value(both), table)
-            out_ref[2 * k, f] = got[:, :LANES]
-            out_ref[2 * k + 1, f] = got[:, LANES:]
+            sbuf[2 * k, f] = got[:, :LANES]
+            sbuf[2 * k + 1, f] = got[:, LANES:]
+        leave += deal(
+            lambda peer, f=f: sbuf.at[peer, f], out_ref.at[me, f], bsend.at[f], brecv.at[f], loc.at[2 + f]
+        )
+    for copy in leave:
+        copy.wait()
 
 
 def turn(x, sign):
     return pltpu.roll(x, LANES // 2, 1) * sign
 
 
-def middle_kernel(rows_total, x_ref, smooth_ref, fh, fl, ih, il, tw_ref, out_ref):
+def middle_kernel(rows_total, x_ref, smooth_ref, fh, fl, ih, il, tw_ref, out_ref, sbuf, send, recv, loc):
     length = rows_total
     radix = length // LANES
     h = radix // 2
     half = LANES // 2
-    me = lax.axis_index("row") * lax.axis_size("col") + lax.axis_index("col")
+    count, me, at = place()
+    greet(count, at)
     lane = lax.broadcasted_iota(jnp.int32, (LANES, LANES), 1)
     row = lax.broadcasted_iota(jnp.int32, (LANES, LANES), 0)
     sign = jnp.where(lane < half, -1.0, 1.0)
@@ -236,7 +298,9 @@
         x = c
         if s is not None:
             x = c + turn(s, sign) if n == j else c - turn(s, sign)
-        out_ref[n] = x
+        sbuf[n] = x
+    for copy in deal(lambda peer: sbuf.at[peer], out_ref.at[me], send, recv, loc.at[0]):
+        copy.wait()
 
 
 def inverse_y_kernel(z_ref, bh, bl, fh, fl, tc, ts, out_ref, sq_ref, top_ref, bot_ref):
@@ -431,22 +495,32 @@
     base, first, inv, first_inv, tc, ts = y_tables(ny)
     fwd_x, inv_x, tw_x = x_tables(nx)
     tc, ts, tw_x = (jnp.asarray(t.astype(np.float32)) for t in (tc, ts, tw_x))
-    x = shear.reshape(2, ncol, rows, cols_in)
-    x = lax.all_to_all(x, "col", split_axis=1, concat_axis=1, tiled=True)
-    x = call(forward_y_kernel, shape(count, 2, rows, LANES), [VM] * 7)(
-        x, *split_table(base), *split_table(first), tc, ts
-    )
-    x = lax.all_to_all(x, GROUP, split_axis=0, concat_axis=0, tiled=True)
-    x = call(partial(middle_kernel, nx), shape(count, rows, LANES), [VM, SM] + [VM] * 5)(
-        x, smoothing, *split_table(fwd_x), *split_table(inv_x), tw_x
-    )
-    x = lax.all_to_all(x, GROUP, split_axis=0, concat_axis=0, tiled=True)
+    dma = pltpu.SemaphoreType.DMA
+    x = call(
+        forward_y_kernel,
+        shape(count, 2, rows, LANES),
+        [pl.BlockSpec(memory_space=pl.ANY)] + [VM] * 6,
+        [
+            pltpu.VMEM((2, ncol, rows, cols_in), F32),
+            pltpu.VMEM((count, 2, rows, LANES), F32),
+            dma((2, ncol)), dma((2, ncol)), dma((2, count)), dma((2, count)), dma((4,)),
+        ],
+        collective_id=2,
+        has_side_effects=True,
+    )(shear, *split_table(base), *split_table(first), tc, ts)
+    x = call(
+        partial(middle_kernel, nx),
+        shape(count, rows, LANES),
+        [VM, SM] + [VM] * 5,
+        [pltpu.VMEM((count, rows, LANES), F32), dma((count,)), dma((count,)), dma((1,))],
+        collective_id=3,
+        has_side_effects=True,
+    )(x, smoothing, *split_table(fwd_x), *split_table(inv_x), tw_x)
     kappa, sq, top, bot = call(
         inverse_y_kernel,
         (shape(rows, ny), shape(1, LANES), shape(1, ny), shape(1, ny)),
         [VM] * 7,
     )(x, *split_table(inv), *split_table(first_inv), tc, ts)
-    dma = pltpu.SemaphoreType.DMA
     slots = [pltpu.VMEM((count - 1, 1, LANES), F32), dma((count - 1,)), dma((count - 1,))]
     sq, above, below = call(
         edge_kernel,

time: 169 us -> 157 us (0.929)
  Pallas kernels: 24.9 us -> 148 us
  blocking collectives: 84.4 us -> 0 us
  waiting for transfers between devices: 48.6 us -> 0 us
  starting transfers between devices: 4.08 us -> 0 us
  local copies, waits for them, and re-layouts: 4.79 us -> 7.16 us
    pallas_call x1, Pallas kernels: 1.32 us -> 93.1 us  [one_map(): call(forward_y_kernel, shape(count, 2, rows, LANES), [pl.BlockSpec(memory...]
    all_to_all x2 -> x0, blocking collectives: 84.4 us -> none  [the longest x1 54.3 us: one_map(): x = lax.all_to_all(x, 'col', split_axis=1, concat_axis=1, tiled=True)]
    all_to_all x1 -> x0, waiting for transfers between devices: 48.6 us -> none  [one_map(): x = lax.all_to_all(x, GROUP, split_axis=0, concat_axis=0, tiled=True)]
    pallas_call x1, Pallas kernels: 5.66 us -> 32.3 us  [one_map(): call(partial(middle_kernel, nx), shape(count, rows, LANES), [VM, SM] + [V...]
    unnamed x37 -> x41, local copies, waits for them, and re-layouts: 2.79 us -> 7.16 us
    pallas_call x1, Pallas kernels: 6.86 us -> 11.1 us  [one_map(): call(edge_kernel, (shape(1, LANES), shape(1, ny), shape(1, ny)), [VM] * 3...]
    all_to_all x1 -> x0, starting transfers between devices: 4.08 us -> none  [one_map(): x = lax.all_to_all(x, GROUP, split_axis=0, concat_axis=0, tiled=True)]
    another operation x1 -> x0, local copies, waits for them, and re-layouts: 1.82 us -> none  [one_map(): x = shear.reshape(2, ncol, rows, cols_in)]
  transfers between devices with their start and end apart: 1 -> 0, of which waited for: 1 -> 0; matrix products, arithmetic and copies ran while one was open for 0% -> 0% of each run, Pallas kernels for 0% -> 0%
where the time goes in v2:
time: 157 us; the launch traced here: 156 us
  Pallas kernels  148 us (94%)
  local copies, waits for them, and re-layouts  7.16 us (5%)
    pallas_call x1, Pallas kernels, one_map(): call(forward_y_kernel, shape(count, 2, rows, LANES), [pl.BlockSpec(memory...  93.1 us
    pallas_call x1, Pallas kernels, one_map(): call(partial(middle_kernel, nx), shape(count, rows, LANES), [VM, SM] + [V...  32.3 us
    pallas_call x1, Pallas kernels, one_map(): call(edge_kernel, (shape(1, LANES), shape(1, ny), shape(1, ny)), [VM] * 3...  11.1 us
    unnamed x41, local copies, waits for them, and re-layouts  7.16 us
    pallas_call x1, Pallas kernels, one_map(): call(sum_kernel, shape(1, LANES), [VM], slots, collective_id=1, has_side_...  6.61 us
    pallas_call x1, Pallas kernels, one_map(): call(partial(peak_kernel, float(nx * ny)), (shape(rows, ny), shape(*offse...  3.55 us

profile of v2, /device:TPU:0, one launch (start us, length us, event | category | flops | bytes accessed | tf_op | source)
XLA Modules:
  0.0 156.3 jit_solution(12365769411044930752)
XLA Ops:
  1.3 0.0 copy-start
  1.3 1.6 %copy-done = f32[2,1,512,512]{3,2,1,0:T(8,128)S(1)} copy-done((f32[2,1,512,512]{3,2,1,0:T(8,128)S(1)}, f32[2,1,512,512]{3,2,1,0:T(8,128)}, u32[]{:S(2)}) %copy-start) | copy-done | bytes 2097176
  2.9 0.0 copy-start.5
  2.9 0.9 copy-done.5
  3.8 0.0 copy-start.6
  3.8 0.9 copy-done.6
  4.7 0.0 copy-start.7
  4.7 0.9 copy-done.7
  5.6 0.0 copy-start.8
  5.6 0.9 copy-done.8
  6.5 0.0 copy-start.14
  6.5 0.7 copy-done.14
  7.2 0.0 copy-start.16
  7.2 0.7 copy-done.16
  7.9 0.0 copy-start.9
  7.9 0.0 copy-start.10
  7.9 0.0 copy-start.11
  7.9 0.0 copy-start.12
  7.9 0.0 copy-start.13
  7.9 93.1 %shard_map.148.x_ref = f32[16,2,128,128]{3,2,1,0:T(8,128)S(1)} custom-call(f32[2,512,512]{2,1,0:T(8,128)S(1)} %bitcast.6, bf16[256,256]{1,0:T(8,128)(2,1)S(1)} %copy-done.8, bf16[256,256]{1,0:T(8,128)(2,1)S(1)} %copy-done.7, bf16[256,256]{1,0:T(8,128)(2,1)S(1)} %copy-done.6, bf16[256,256]{1,0:T(8,128)(2,1)S(1)} %copy-done.5, f32[8,128]{1,0:T(8,128)S(1)} %copy-done.16, ...), custom_call_target="tpu_custom_call" | custom-call | tf_op jit(solution)/shard_map/pallas_call | solution.py:499
  101.0 0.0 copy-done.9
  101.0 0.0 copy-done.10
  101.0 0.0 copy-done.11
  101.0 0.0 copy-done.12
  101.0 0.0 copy-done.13
  101.0 0.0 copy-start.1
  101.0 0.0 copy-start.2
  101.0 0.0 copy-start.3
  101.1 0.0 copy-start.4
  101.1 0.0 copy-start.15
  101.1 0.0 copy-start.17
  101.1 0.0 copy-start.18
  101.1 0.0 copy-start.19
  101.1 32.3 %shard_map.149.z_ref = f32[16,128,128]{2,1,0:T(8,128)S(1)} custom-call(f32[16,2,128,128]{3,2,1,0:T(8,128)S(1)} %shard_map.148.x_ref, f32[1]{0:T(128)S(6)} %copy.17.smooth_ref, bf16[128,256]{1,0:T(8,128)(2,1)S(1)} %copy-done.12, bf16[128,256]{1,0:T(8,128)(2,1)S(1)} %copy-done.11, bf16[128,256]{1,0:T(8,128)(2,1)S(1)} %copy-done.10, ...), custom_call_target="tpu_custom_call" | custom-call | tf_op jit(solution)/shard_map/pallas_call | solution.py:511
  133.4 0.0 copy-done.1
  133.4 0.0 copy-done.2
  133.5 0.0 copy-done.3
  133.5 0.0 copy-done.4
  133.5 0.0 copy-done.15
  133.5 0.0 copy-done.17
  133.5 1.0 shard_map.150
  134.5 11.1 %shard_map.151 = (f32[1,128]{1,0:T(1,128)S(1)}, f32[1,2048]{1,0:T(1,128)S(1)}, f32[1,2048]{1,0:T(1,128)S(1)}) custom-call(f32[1,128]{1,0:T(1,128)S(1)} %get-tuple-element.14.sq_ref, f32[1,2048]{1,0:T(1,128)S(1)} %get-tuple-element.15.top_ref, f32[1,2048]{1,0:T(1,128)S(1)} %get-tuple-element.16.bot_ref), custom_call_target="tpu_custom_call" | custom-call | tf_op jit(solution)/shard_map/pallas_call | solution.py:525
  145.6 0.0 copy-done.18
  145.6 0.0 copy-done.19
  145.6 3.5 %shard_map.152 = (f32[128,2048]{1,0:T(8,128)}, f32[8,128]{1,0:T(8,128)}, f32[1,128]{1,0:T(1,128)S(1)}) custom-call(f32[128,2048]{1,0:T(8,128)S(1)} %get-tuple-element.13.x_ref, f32[1,2048]{1,0:T(1,128)S(1)} %get-tuple-element.17.above_ref, f32[1,2048]{1,0:T(1,128)S(1)} %get-tuple-element.18.below_ref, f32[1,128]{1,0:T(1,128)S(1)} %get-tuple-element.19.sq_ref, ...), custom_call_target="tpu_custom_call" | custom-call | tf_op jit(solution)/shard_map/pallas_call | solution.py:533
  149.2 6.6 %shard_map.153 = f32[1,128]{1,0:T(1,128)S(1)} custom-call(f32[1,128]{1,0:T(1,128)S(1)} %get-tuple-element.22.x_ref), custom_call_target="tpu_custom_call" | custom-call | tf_op jit(solution)/shard_map/pallas_call | solution.py:539
  155.8 0.5 copy.18
Async XLA Ops:
  1.3 1.6 %copy-start = (f32[2,1,512,512]{3,2,1,0:T(8,128)S(1)}, f32[2,1,512,512]{3,2,1,0:T(8,128)}, u32[]{:S(2)}) copy-start(f32[2,1,512,512]{3,2,1,0:T(8,128)} %param.13) | copy-start | bytes 6291460
  2.9 0.9 copy-start.5
  3.8 0.9 copy-start.6
  4.7 0.9 copy-start.7
  5.6 0.9 copy-start.8
  6.5 0.7 copy-start.14
  7.2 0.7 copy-start.16
  7.9 93.1 %copy-start.9 = (bf16[128,256]{1,0:T(8,128)(2,1)S(1)}, bf16[128,256]{1,0:T(8,128)(2,1)}, u32[]{:S(2)}) copy-start(bf16[128,256]{1,0:T(8,128)(2,1)} %constant.46.il) | copy-start | bytes 196612
  7.9 93.1 %copy-start.10 = (bf16[128,256]{1,0:T(8,128)(2,1)S(1)}, bf16[128,256]{1,0:T(8,128)(2,1)}, u32[]{:S(2)}) copy-start(bf16[128,256]{1,0:T(8,128)(2,1)} %constant.43.ih) | copy-start | bytes 196612
  7.9 93.1 %copy-start.11 = (bf16[128,256]{1,0:T(8,128)(2,1)S(1)}, bf16[128,256]{1,0:T(8,128)(2,1)}, u32[]{:S(2)}) copy-start(bf16[128,256]{1,0:T(8,128)(2,1)} %constant.42.fl) | copy-start | bytes 196612
  7.9 93.1 %copy-start.12 = (bf16[128,256]{1,0:T(8,128)(2,1)S(1)}, bf16[128,256]{1,0:T(8,128)(2,1)}, u32[]{:S(2)}) copy-start(bf16[128,256]{1,0:T(8,128)(2,1)} %constant.39.fh) | copy-start | bytes 196612
  7.9 93.1 %copy-start.13 = (f32[128,32]{1,0:T(8,128)S(1)}, f32[128,32]{1,0:T(8,128)}, u32[]{:S(2)}) copy-start(f32[128,32]{1,0:T(8,128)} %constant.20.clone.tw_ref) | copy-start | bytes 49156
  101.0 32.4 %copy-start.1 = (bf16[256,256]{1,0:T(8,128)(2,1)S(1)}, bf16[256,256]{1,0:T(8,128)(2,1)}, u32[]{:S(2)}) copy-start(bf16[256,256]{1,0:T(8,128)(2,1)} %constant.54.fl) | copy-start | bytes 393220
  101.0 32.4 %copy-start.2 = (bf16[256,256]{1,0:T(8,128)(2,1)S(1)}, bf16[256,256]{1,0:T(8,128)(2,1)}, u32[]{:S(2)}) copy-start(bf16[256,256]{1,0:T(8,128)(2,1)} %constant.51.fh) | copy-start | bytes 393220
  101.0 32.4 %copy-start.3 = (bf16[256,256]{1,0:T(8,128)(2,1)S(1)}, bf16[256,256]{1,0:T(8,128)(2,1)}, u32[]{:S(2)}) copy-start(bf16[256,256]{1,0:T(8,128)(2,1)} %constant.50.bl) | copy-start | bytes 393220
  101.1 32.4 %copy-start.4 = (bf16[256,256]{1,0:T(8,128)(2,1)S(1)}, bf16[256,256]{1,0:T(8,128)(2,1)}, u32[]{:S(2)}) copy-start(bf16[256,256]{1,0:T(8,128)(2,1)} %constant.47.bh) | copy-start | bytes 393220
  101.1 32.4 %copy-start.15 = (f32[8,128]{1,0:T(8,128)S(1)}, f32[8,128]{1,0:T(8,128)}, u32[]{:S(2)}) copy-start(f32[8,128]{1,0:T(8,128)} %constant.19.clone.ts) | copy-start | bytes 12292
  101.1 32.4 %copy-start.17 = (f32[8,128]{1,0:T(8,128)S(1)}, f32[8,128]{1,0:T(8,128)}, u32[]{:S(2)}) copy-start(f32[8,128]{1,0:T(8,128)} %constant.18.clone.tc) | copy-start | bytes 12292
  101.1 44.5 %copy-start.18 = (s32[1,8,128]{2,1,0:T(8,128)S(1)}, s32[1,8,128]{2,1,0:T(8,128)}, u32[]{:S(2)}) copy-start(s32[1,8,128]{2,1,0:T(8,128)} %param.15) | copy-start | bytes 12292
  101.1 44.5 %copy-start.19 = (s32[1,16]{1,0:T(1,128)S(1)}, s32[1,16]{1,0:T(1,128)}, u32[]{:S(2)}) copy-start(s32[1,16]{1,0:T(1,128)} %param.16) | copy-start | bytes 196

commit v3 on v2

--- a/solution.py
+++ b/solution.py
@@ -162,11 +162,8 @@
     return copies + [own]
 
 
-def forward_y_kernel(shear, bh, bl, fh, fl, tc, ts, out_ref, xbuf, sbuf, asend, arecv, bsend, brecv, loc):
-    _, cols, rows, width = xbuf.shape
-    per = width // LANES
-    count, me, at = place()
-    greet(count, at)
+def start_shear(shear, xbuf, asend, arecv, loc):
+    _, cols, rows, _ = xbuf.shape
     here = lax.axis_index("col")
     arrive = []
     for f in range(2):
@@ -185,7 +182,14 @@
             copy.start()
             copies.append(copy)
         arrive.append(copies)
-    base, first = (bh[...], bl[...]), (fh[...], fl[...])
+    return arrive
+
+
+def forward_y(arrive, xbuf, tables, tc, ts, out_ref, sbuf, bsend, brecv, loc):
+    _, cols, rows, width = xbuf.shape
+    per = width // LANES
+    _, me, _ = place()
+    base, first = ((high[...], low[...]) for high, low in tables)
     leave = []
     for f in range(2):
         for copy in arrive[f]:
@@ -206,7 +210,7 @@
             sbuf[2 * k, f] = got[:, :LANES]
             sbuf[2 * k + 1, f] = got[:, LANES:]
         leave += deal(
-            lambda peer, f=f: sbuf.at[peer, f], out_ref.at[me, f], bsend.at[f], brecv.at[f], loc.at[2 + f]
+            lambda peer, f=f: sbuf.at[peer, f], out_ref.at[me, f], bsend.at[f], brecv.at[f], loc.at[f]
         )
     for copy in leave:
         copy.wait()
@@ -216,13 +220,12 @@
     return pltpu.roll(x, LANES // 2, 1) * sign
 
 
-def middle_kernel(rows_total, x_ref, smooth_ref, fh, fl, ih, il, tw_ref, out_ref, sbuf, send, recv, loc):
-    length = rows_total
+def middle(length, x_ref, smooth_ref, fwd, inv, tw_ref, out_ref, sbuf, send, recv, loc):
+    fwd, inv = (fwd[0][...], fwd[1][...]), (inv[0][...], inv[1][...])
     radix = length // LANES
     h = radix // 2
     half = LANES // 2
-    count, me, at = place()
-    greet(count, at)
+    _, me, _ = place()
     lane = lax.broadcasted_iota(jnp.int32, (LANES, LANES), 1)
     row = lax.broadcasted_iota(jnp.int32, (LANES, LANES), 0)
     sign = jnp.where(lane < half, -1.0, 1.0)
@@ -244,7 +247,6 @@
     corner = jnp.sum(total * alternate, axis=0, keepdims=True)
     two = [jnp.where(packed, -sign * a, b) for a, b in zip(one, two_raw)]
     sums = (cos_sin_sums(one), cos_sin_sums(two))
-    fwd, inv = (fh[...], fl[...]), (ih[...], il[...])
     width = smooth_ref[0]
     scale = -2.0 * math.pi**2 * width * width
     edge = -float(length // 2)
@@ -303,11 +305,11 @@
         copy.wait()
 
 
-def inverse_y_kernel(z_ref, bh, bl, fh, fl, tc, ts, out_ref, sq_ref, top_ref, bot_ref):
+def inverse_y(z_ref, tables, tc, ts, out_ref, sq_ref, top_ref, bot_ref):
     count, rows, _ = z_ref.shape
     h = count // 2
     radix = count
-    base, first = (bh[...], bl[...]), (fh[...], fl[...])
+    base, first = ((high[...], low[...]) for high, low in tables)
     real, imag = [None] * (h + 1), [None] * (h + 1)
     for k in range(h):
         both = jnp.concatenate([z_ref[2 * k], z_ref[2 * k + 1]], axis=1)
@@ -371,48 +373,35 @@
     return copies
 
 
-def sum_kernel(x_ref, out_ref, slots, send, recv):
+def gather_sum(copies, own, slots):
+    for copy in copies:
+        copy.wait()
+    total = own[...]
+    for d in range(slots.shape[0]):
+        total = total + slots[d]
+    return total
+
+
+def peaks(pixels, x_ref, sq_ref, top_ref, bot_ref, off_ref, thr_ref, rms_ref, high_ref, cnt_ref,
+          cnt_own, wide, above_ref, below_ref, slots, send, recv, hsend, hrecv):
+    rows, width = x_ref.shape
+    cells = width // CELL
+    pad = 8
     count, _, at = place()
-    greet(count, at)
-    for copy in spread(count, at, x_ref, slots, send, recv):
-        copy.wait()
-    total = x_ref[...]
-    for d in range(1, count):
-        total = total + slots[d - 1]
-    out_ref[...] = total
-
-
-def edge_kernel(sq_ref, top_ref, bot_ref, out_ref, above_ref, below_ref, slots, send, recv, hsend, hrecv):
-    count, _, at = place()
-    greet(count, at)
-    copies = spread(count, at, sq_ref, slots, send, recv)
+    copies = spread(count, at, sq_ref, slots.at[0], send.at[0], recv.at[0])
+    edges = []
     for i, (src, dst, d) in enumerate(((bot_ref, above_ref, 1), (top_ref, below_ref, count - 1))):
         copy = pltpu.make_async_remote_copy(
             src_ref=src, dst_ref=dst, send_sem=hsend.at[i], recv_sem=hrecv.at[i],
             device_id=at(d), device_id_type=MESH,
         )
         copy.start()
-        copies.append(copy)
-    for copy in copies:
-        copy.wait()
-    total = sq_ref[...]
-    for d in range(1, count):
-        total = total + slots[d - 1]
-    out_ref[...] = total
-
-
-def peak_kernel(pixels, x_ref, above_ref, below_ref, sq_ref, off_ref, thr_ref, snr_ref, high_ref, cnt_ref, wide):
-    rows, width = x_ref.shape
-    cells = width // CELL
-    pad = 8
-    rms = jnp.sqrt(jnp.sum(sq_ref[...], axis=1, keepdims=True) / pixels + 1e-06)
+        edges.append(copy)
 
     def three(x):
         side = jnp.maximum(pltpu.roll(x, 1, 1), pltpu.roll(x, width - 1, 1))
         return side, jnp.maximum(side, x)
 
-    wide[pad - 1 : pad, :] = three(jnp.broadcast_to(above_ref[...], (8, width)))[1][:1]
-    wide[pad + rows : pad + rows + 1, :] = three(jnp.broadcast_to(below_ref[...], (8, width)))[1][:1]
     for p in range(rows // CELL):
         sl = slice(p * CELL, (p + 1) * CELL)
         wide[pad + p * CELL : pad + (p + 1) * CELL, :] = three(x_ref[sl, :])[1]
@@ -427,10 +416,13 @@
         lax.broadcasted_iota(jnp.int32, (CELL, width), 1) % CELL
     )
     tops, mids = [], []
+    for copy in edges:
+        copy.wait()
+    wide[pad - 1 : pad, :] = three(jnp.broadcast_to(above_ref[...], (8, width)))[1][:1]
+    wide[pad + rows : pad + rows + 1, :] = three(jnp.broadcast_to(below_ref[...], (8, width)))[1][:1]
     for p in range(rows // CELL):
         low = pad + p * CELL
         x = x_ref[p * CELL : (p + 1) * CELL, :]
-        snr_ref[p * CELL : (p + 1) * CELL, :] = x / rms
         near = jnp.maximum(
             three(x)[0],
             jnp.maximum(wide[low - 1 : low - 1 + CELL, :], wide[low + 1 : low + 1 + CELL, :]),
@@ -451,8 +443,11 @@
         c = (rest - b.astype(jnp.float32)).astype(jnp.bfloat16)
         return dot(a, spread_table) + (dot(b, spread_table) + dot(c, spread_table))
 
-    heights = gather(tops) / rms
-    values = gather(mids) / rms
+    heights, values = gather(tops), gather(mids)
+    square = gather_sum(copies, sq_ref, slots.at[0])
+    rms = jnp.sqrt(jnp.sum(square, axis=1, keepdims=True) / pixels + 1e-06)
+    rms_ref[...] = jnp.broadcast_to(rms, (1, LANES))
+    heights, values = heights / rms, values / rms
     high_ref[...] = heights
     weight = 1.0 / (1.0 + jnp.exp(-heights / PEAK_SOFT))
     lane = lax.broadcasted_iota(jnp.int32, (1, LANES), 1)
@@ -462,28 +457,49 @@
         above = weight / (1.0 + jnp.exp((level - values) / BIN_SOFT))
         one = jnp.sum(jnp.sum(above, axis=0, keepdims=True), axis=1, keepdims=True)
         counts = jnp.where(lane == k, one, counts)
-    cnt_ref[...] = counts
+    cnt_own[...] = counts
+    copies = spread(count, at, cnt_own, slots.at[1], send.at[1], recv.at[1])
+    cnt_ref[...] = gather_sum(copies, cnt_own, slots.at[1])
+
+
+def kernel(sizes, shear, smooth_ref, off_hbm, thr_ref, wide_hbm, thin_hbm,
+           x_ref, rms_ref, high_ref, cnt_ref,
+           xbuf, sbuf, spec, field, zbuf, wide, off_ref, table, thin, sq_ref, cnt_own,
+           top_ref, bot_ref, above_ref, below_ref, slots,
+           asend, arecv, bsend, brecv, csend, crecv, esend, erecv, hsend, hrecv, loc):
+    nx, ny = sizes
+    count, _, at = place()
+    extra = [
+        pltpu.make_async_copy(src, dst, loc.at[i])
+        for i, (src, dst) in enumerate(((wide_hbm, table), (thin_hbm, thin), (off_hbm, off_ref)))
+    ]
+    for copy in extra:
+        copy.start()
+    greet(count, at)
+    arrive = start_shear(shear, xbuf, asend, arecv, loc.at[pl.ds(3, 2)])
+    for copy in extra:
+        copy.wait()
+    full, part = 2 * LANES, LANES
+    starts = [i * full for i in range(8)] + [8 * full + i * part for i in range(4)]
+    sizes_of = [full] * 8 + [part] * 4
+    t = [table.at[a : a + n] for a, n in zip(starts, sizes_of)]
+    h = nx // LANES // 2
+    tc, ts, tw = thin.at[0:h], thin.at[h : 2 * h], thin.at[2 * h : 2 * h + LANES]
+    forward_y(arrive, xbuf, ((t[0], t[1]), (t[2], t[3])), tc, ts, spec, sbuf, bsend, brecv, loc.at[pl.ds(5, 2)])
+    middle(nx, spec, smooth_ref, (t[8], t[9]), (t[10], t[11]), tw, zbuf, field, csend, crecv, loc.at[pl.ds(7, 1)])
+    inverse_y(zbuf, ((t[4], t[5]), (t[6], t[7])), tc, ts, x_ref, sq_ref, top_ref, bot_ref)
+    peaks(float(nx * ny), x_ref, sq_ref, top_ref, bot_ref, off_ref, thr_ref, rms_ref, high_ref, cnt_ref,
+          cnt_own, wide, above_ref, below_ref, slots, esend, erecv, hsend, hrecv)
 
 
 VM = pl.BlockSpec(memory_space=pltpu.VMEM)
+HB = pl.BlockSpec(memory_space=pltpu.HBM)
 SM = pl.BlockSpec(memory_space=pltpu.SMEM)
 F32 = jnp.float32
 
 
 def shape(*dims):
     return jax.ShapeDtypeStruct(dims, F32)
-
-
-def call(kernel, out_shape, specs, scratch=(), **params):
-    outs = out_shape if isinstance(out_shape, tuple) else None
-    return pl.pallas_call(
-        kernel,
-        out_shape=out_shape,
-        in_specs=specs,
-        out_specs=VM if outs is None else tuple(VM for _ in outs),
-        scratch_shapes=list(scratch),
-        compiler_params=pltpu.CompilerParams(vmem_limit_bytes=40 * 2**20, **params),
-    )
 
 
 def one_map(shear, smoothing, offsets, thresholds):
@@ -494,52 +510,38 @@
     rows = nx // count
     base, first, inv, first_inv, tc, ts = y_tables(ny)
     fwd_x, inv_x, tw_x = x_tables(nx)
-    tc, ts, tw_x = (jnp.asarray(t.astype(np.float32)) for t in (tc, ts, tw_x))
+    parts = [half for t in (base, first, inv, first_inv, fwd_x, inv_x) for half in split_table(t)]
+    table = jnp.concatenate(parts, axis=0)
+    tw_x = np.pad(tw_x, ((0, 0), (0, LANES - tw_x.shape[1])))
+    thin = jnp.asarray(np.concatenate([tc, ts, tw_x], axis=0).astype(np.float32))
     dma = pltpu.SemaphoreType.DMA
-    x = call(
-        forward_y_kernel,
-        shape(count, 2, rows, LANES),
-        [pl.BlockSpec(memory_space=pl.ANY)] + [VM] * 6,
-        [
-            pltpu.VMEM((2, ncol, rows, cols_in), F32),
-            pltpu.VMEM((count, 2, rows, LANES), F32),
-            dma((2, ncol)), dma((2, ncol)), dma((2, count)), dma((2, count)), dma((4,)),
+    vm = lambda *dims: pltpu.VMEM(dims, F32)
+    kappa, rms, heights, counts = pl.pallas_call(
+        partial(kernel, (nx, ny)),
+        out_shape=(shape(rows, ny), shape(1, LANES), shape(*offsets.shape), shape(1, LANES)),
+        in_specs=[HB, SM, HB, SM, HB, HB],
+        out_specs=(VM, VM, VM, VM),
+        scratch_shapes=[
+            vm(2, ncol, rows, cols_in),
+            vm(count, 2, rows, LANES),
+            vm(count, 2, rows, LANES),
+            vm(count, rows, LANES),
+            vm(count, rows, LANES),
+            vm(rows + 16, ny),
+            pltpu.VMEM(offsets.shape, jnp.int32),
+            pltpu.VMEM(table.shape, jnp.bfloat16),
+            vm(*thin.shape),
+            vm(1, LANES), vm(1, LANES),
+            vm(1, ny), vm(1, ny), vm(1, ny), vm(1, ny),
+            vm(2, count - 1, 1, LANES),
+            dma((2, ncol)), dma((2, ncol)), dma((2, count)), dma((2, count)), dma((count,)), dma((count,)),
+            dma((2, count - 1)), dma((2, count - 1)), dma((2,)), dma((2,)), dma((8,)),
         ],
-        collective_id=2,
-        has_side_effects=True,
-    )(shear, *split_table(base), *split_table(first), tc, ts)
-    x = call(
-        partial(middle_kernel, nx),
-        shape(count, rows, LANES),
-        [VM, SM] + [VM] * 5,
-        [pltpu.VMEM((count, rows, LANES), F32), dma((count,)), dma((count,)), dma((1,))],
-        collective_id=3,
-        has_side_effects=True,
-    )(x, smoothing, *split_table(fwd_x), *split_table(inv_x), tw_x)
-    kappa, sq, top, bot = call(
-        inverse_y_kernel,
-        (shape(rows, ny), shape(1, LANES), shape(1, ny), shape(1, ny)),
-        [VM] * 7,
-    )(x, *split_table(inv), *split_table(first_inv), tc, ts)
-    slots = [pltpu.VMEM((count - 1, 1, LANES), F32), dma((count - 1,)), dma((count - 1,))]
-    sq, above, below = call(
-        edge_kernel,
-        (shape(1, LANES), shape(1, ny), shape(1, ny)),
-        [VM] * 3,
-        slots + [dma((2,)), dma((2,))],
-        collective_id=0,
-        has_side_effects=True,
-    )(sq, top, bot)
-    snr, heights, local = call(
-        partial(peak_kernel, float(nx * ny)),
-        (shape(rows, ny), shape(*offsets.shape), shape(1, LANES)),
-        [VM] * 5 + [SM],
-        [pltpu.VMEM((rows + 16, ny), F32)],
-    )(kappa, above, below, sq, offsets, thresholds)
-    counts = call(
-        sum_kernel, shape(1, LANES), [VM], slots, collective_id=1, has_side_effects=True
-    )(local)
-    return snr, heights, counts[0, : thresholds.shape[0]]
+        compiler_params=pltpu.CompilerParams(
+            vmem_limit_bytes=48 * 2**20, collective_id=0, has_side_effects=True
+        ),
+    )(shear, smoothing, offsets, thresholds, table, thin)
+    return kappa / rms[:, :1], heights, counts[0, : thresholds.shape[0]]
 
 
 def body(shear, smoothing, offsets, thresholds):

time: 157 us -> 145 us (0.924)
  Pallas kernels: 148 us -> 136 us
    pallas_call x6 -> x1, Pallas kernels: 148 us -> 136 us  [one_map(): pl.pallas_call(partial(kernel, (nx, ny)), out_shape=(shape(rows, ny), sha...]
    unnamed x41 -> x12, local copies, waits for them, and re-layouts: 7.16 us -> 6.23 us
where the time goes in v3:
time: 145 us
  Pallas kernels  136 us (94%)
  local copies, waits for them, and re-layouts  6.23 us (4%)
    pallas_call x1, Pallas kernels, one_map(): pl.pallas_call(partial(kernel, (nx, ny)), out_shape=(shape(rows, ny), sha...  136 us
    unnamed x12, local copies, waits for them, and re-layouts  6.23 us

profile of v3, /device:TPU:0, one launch (start us, length us, event | category | flops | bytes accessed | tf_op | source)
XLA Modules:
  0.0 144.7 jit_solution(5055784395107607370)
XLA Ops:
  1.3 0.0 copy-start
  1.3 1.6 %copy-done = f32[2,1,512,512]{3,2,1,0:T(8,128)S(1)} copy-done((f32[2,1,512,512]{3,2,1,0:T(8,128)S(1)}, f32[2,1,512,512]{3,2,1,0:T(8,128)}, u32[]{:S(2)}) %copy-start) | copy-done | bytes 2097176
  2.9 0.0 copy-start.1
  2.9 1.3 copy-done.1
  4.2 0.0 copy-start.2
  4.2 0.9 copy-done.2
  5.1 0.0 copy-start.3
  5.1 0.7 copy-done.3
  5.8 0.0 copy-start.4
  5.8 0.7 copy-done.4
  6.4 136.0 %shard_map.130 = (f32[128,2048]{1,0:T(8,128)S(1)}, f32[1,128]{1,0:T(1,128)S(1)}, f32[8,128]{1,0:T(8,128)S(1)}, f32[1,128]{1,0:T(1,128)S(1)}) custom-call(f32[2,512,512]{2,1,0:T(8,128)S(1)} %bitcast.9, f32[1]{0:T(128)S(6)} %copy.16.smooth_ref, s32[8,128]{1,0:T(8,128)S(1)} %bitcast.10, s32[16]{0:T(128)S(1)} %bitcast.12, bf16[2560,256]{1,0:T(8,128)(2,1)S(1)} %copy-done.1, ...), custom_call_target="tpu_custom_call" | custom-call | tf_op jit(solution)/shard_map/pallas_call | solution.py:519
  142.4 1.1 divide_bitcast_fusion
  143.6 0.6 copy.17
  144.2 0.5 copy.18
Async XLA Ops:
  1.3 1.6 %copy-start = (f32[2,1,512,512]{3,2,1,0:T(8,128)S(1)}, f32[2,1,512,512]{3,2,1,0:T(8,128)}, u32[]{:S(2)}) copy-start(f32[2,1,512,512]{3,2,1,0:T(8,128)} %param.11) | copy-start | bytes 6291460
  2.9 1.3 copy-start.1
  4.2 0.9 copy-start.2
  5.1 0.7 copy-start.3
  5.8 0.7 copy-start.4

commit v4 on v3

--- a/solution.py
+++ b/solution.py
@@ -212,15 +212,14 @@
         leave += deal(
             lambda peer, f=f: sbuf.at[peer, f], out_ref.at[me, f], bsend.at[f], brecv.at[f], loc.at[f]
         )
-    for copy in leave:
-        copy.wait()
+    return leave[: len(leave) // 2], leave[len(leave) // 2 :]
 
 
 def turn(x, sign):
     return pltpu.roll(x, LANES // 2, 1) * sign
 
 
-def middle(length, x_ref, smooth_ref, fwd, inv, tw_ref, out_ref, sbuf, send, recv, loc):
+def middle(length, leave, gbuf, x_ref, smooth_ref, fwd, inv, tw_ref, out_ref, sbuf, send, recv, loc):
     fwd, inv = (fwd[0][...], fwd[1][...]), (inv[0][...], inv[1][...])
     radix = length // LANES
     h = radix // 2
@@ -238,6 +237,28 @@
     )
     packed = slot == 0
     ky = jnp.where(freq < length // 2, freq, freq - length).astype(jnp.float32)
+    def spectra(k, sums):
+        j = min(k, radix - k)
+        c, s = sums[j]
+        x = c
+        if s is not None:
+            x = c - turn(s, sign) if k == j else c + turn(s, sign)
+        ix = turn(x, sign)
+        if k:
+            wc, ws = tw_ref[:, k : k + 1], tw_ref[:, radix + k : radix + k + 1]
+            x, ix = wc * x - ws * ix, wc * ix + ws * x
+        return jnp.concatenate([x, ix], axis=0)
+
+    for copy in leave[0]:
+        copy.wait()
+    sums = cos_sin_sums([x_ref[n, 0] for n in range(radix)])
+    for k in range(0, radix, 2):
+        pair = jnp.concatenate([spectra(k, sums), spectra(k + 1, sums)], axis=1)
+        got = mm(fwd, split_value(pair))
+        gbuf[k] = got[:, :LANES]
+        gbuf[k + 1] = got[:, LANES:]
+    for copy in leave[1]:
+        copy.wait()
     one = [x_ref[n, 0] for n in range(radix)]
     two_raw = [x_ref[n, 1] for n in range(radix)]
     alternate = jnp.where(row % 2 == 0, 1.0, -1.0)
@@ -246,26 +267,17 @@
         total = total + two_raw[n]
     corner = jnp.sum(total * alternate, axis=0, keepdims=True)
     two = [jnp.where(packed, -sign * a, b) for a, b in zip(one, two_raw)]
-    sums = (cos_sin_sums(one), cos_sin_sums(two))
+    sums = cos_sin_sums(two)
     width = smooth_ref[0]
     scale = -2.0 * math.pi**2 * width * width
     edge = -float(length // 2)
     results = []
     for k in range(radix):
-        j = min(k, radix - k)
         wc, ws = tw_ref[:, k : k + 1], tw_ref[:, radix + k : radix + k + 1]
-        cols = []
-        for f in range(2):
-            c, s = sums[f][j]
-            x = c
-            if s is not None:
-                x = c - turn(s, sign) if k == j else c + turn(s, sign)
-            ix = turn(x, sign)
-            if k:
-                x, ix = wc * x - ws * ix, wc * ix + ws * x
-            cols.append(jnp.concatenate([x, ix], axis=0))
-        got = mm(fwd, split_value(jnp.concatenate(cols, axis=1)))
-        g1, g2 = got[:, :LANES], got[:, LANES:]
+        if k % 2 == 0:
+            pair = jnp.concatenate([spectra(k, sums), spectra(k + 1, sums)], axis=1)
+            both = mm(fwd, split_value(pair))
+        g1, g2 = gbuf[k], both[:, LANES * (k % 2) : LANES * (k % 2 + 1)]
         fx = k + radix * row
         kx = jnp.where(fx < length // 2, fx, fx - length).astype(jnp.float32)
 
@@ -464,7 +476,7 @@
 
 def kernel(sizes, shear, smooth_ref, off_hbm, thr_ref, wide_hbm, thin_hbm,
            x_ref, rms_ref, high_ref, cnt_ref,
-           xbuf, sbuf, spec, field, zbuf, wide, off_ref, table, thin, sq_ref, cnt_own,
+           xbuf, sbuf, spec, gbuf, field, zbuf, wide, off_ref, table, thin, sq_ref, cnt_own,
            top_ref, bot_ref, above_ref, below_ref, slots,
            asend, arecv, bsend, brecv, csend, crecv, esend, erecv, hsend, hrecv, loc):
     nx, ny = sizes
@@ -485,8 +497,8 @@
     t = [table.at[a : a + n] for a, n in zip(starts, sizes_of)]
     h = nx // LANES // 2
     tc, ts, tw = thin.at[0:h], thin.at[h : 2 * h], thin.at[2 * h : 2 * h + LANES]
-    forward_y(arrive, xbuf, ((t[0], t[1]), (t[2], t[3])), tc, ts, spec, sbuf, bsend, brecv, loc.at[pl.ds(5, 2)])
-    middle(nx, spec, smooth_ref, (t[8], t[9]), (t[10], t[11]), tw, zbuf, field, csend, crecv, loc.at[pl.ds(7, 1)])
+    leave = forward_y(arrive, xbuf, ((t[0], t[1]), (t[2], t[3])), tc, ts, spec, sbuf, bsend, brecv, loc.at[pl.ds(5, 2)])
+    middle(nx, leave, gbuf, spec, smooth_ref, (t[8], t[9]), (t[10], t[11]), tw, zbuf, field, csend, crecv, loc.at[pl.ds(7, 1)])
     inverse_y(zbuf, ((t[4], t[5]), (t[6], t[7])), tc, ts, x_ref, sq_ref, top_ref, bot_ref)
     peaks(float(nx * ny), x_ref, sq_ref, top_ref, bot_ref, off_ref, thr_ref, rms_ref, high_ref, cnt_ref,
           cnt_own, wide, above_ref, below_ref, slots, esend, erecv, hsend, hrecv)
@@ -525,6 +537,7 @@
             vm(2, ncol, rows, cols_in),
             vm(count, 2, rows, LANES),
             vm(count, 2, rows, LANES),
+            vm(nx // LANES, LANES, LANES),
             vm(count, rows, LANES),
             vm(count, rows, LANES),
             vm(rows + 16, ny),
@@ -538,7 +551,7 @@
             dma((2, count - 1)), dma((2, count - 1)), dma((2,)), dma((2,)), dma((8,)),
         ],
         compiler_params=pltpu.CompilerParams(
-            vmem_limit_bytes=48 * 2**20, collective_id=0, has_side_effects=True
+            vmem_limit_bytes=63 * 2**20, collective_id=0, has_side_effects=True
         ),
     )(shear, smoothing, offsets, thresholds, table, thin)
     return kappa / rms[:, :1], heights, counts[0, : thresholds.shape[0]]

time: 145 us -> 141 us (0.972)
  local copies, waits for them, and re-layouts: 6.23 us -> 1.11 us
  other arithmetic: 1.12 us -> 2.87 us
    unnamed x12 -> x6, local copies, waits for them, and re-layouts: 6.23 us -> 1.11 us
    another operation x1, other arithmetic: 1.12 us -> 2.87 us  [body(): return tuple((jnp.stack(parts) for parts in zip(*outs)))]
where the time goes in v4:
time: 141 us
  Pallas kernels  136 us (96%)
  other arithmetic  2.87 us (2%)
    pallas_call x1, Pallas kernels, one_map(): pl.pallas_call(partial(kernel, (nx, ny)), out_shape=(shape(rows, ny), sha...  136 us
    another operation x1, other arithmetic, body(): return tuple((jnp.stack(parts) for parts in zip(*outs)))  2.87 us

profile of v4, /device:TPU:0, one launch (start us, length us, event | category | flops | bytes accessed | tf_op | source)
XLA Modules:
  0.0 140.9 jit_solution(4028137015343454505)
XLA Ops:
  1.3 135.6 %shard_map.130 = (f32[128,2048]{1,0:T(8,128)}, f32[1,128]{1,0:T(1,128)}, f32[8,128]{1,0:T(8,128)}, f32[1,128]{1,0:T(1,128)}) custom-call(f32[2,512,512]{2,1,0:T(8,128)} %bitcast.9, f32[1]{0:T(128)S(6)} %copy.16.smooth_ref, s32[8,128]{1,0:T(8,128)} %bitcast.10, s32[16]{0:T(128)} %bitcast.12, bf16[2560,256]{1,0:T(8,128)(2,1)} %constant.49.wide_hbm, ...), custom_call_target="tpu_custom_call" | custom-call | tf_op jit(solution)/shard_map/pallas_call | solution.py:531
  136.9 0.0 copy-start
  136.9 0.0 copy-start.1
  136.9 2.9 %divide_bitcast_fusion = f32[1,128,2048]{2,1,0:T(8,128)} fusion(f32[128,2048]{1,0:T(8,128)} %get-tuple-element.7, f32[]{:T(128)} %bitcast.13), kind=kLoop, calls=%fused_computation | loop fusion | flops 262144 | bytes 2097156 | tf_op jit(solution)/shard_map/stack | solution.py:565
  139.8 0.0 copy-done
  139.8 0.6 copy.17
  140.4 0.0 copy-done.1
  140.4 0.5 copy.18
Async XLA Ops:
  136.9 2.9 %copy-start = (f32[8,128]{1,0:T(8,128)S(1)}, f32[8,128]{1,0:T(8,128)}, u32[]{:S(2)}) copy-start(f32[8,128]{1,0:T(8,128)} %get-tuple-element.9) | copy-start | bytes 12292
  136.9 3.5 %copy-start.1 = (f32[1,128]{1,0:T(1,128)S(1)}, f32[1,128]{1,0:T(1,128)}, u32[]{:S(2)}) copy-start(f32[1,128]{1,0:T(1,128)} %get-tuple-element.10) | copy-start | bytes 1540

commit v5 on v4

--- a/solution.py
+++ b/solution.py
@@ -219,7 +219,7 @@
     return pltpu.roll(x, LANES // 2, 1) * sign
 
 
-def middle(length, leave, gbuf, x_ref, smooth_ref, fwd, inv, tw_ref, out_ref, sbuf, send, recv, loc):
+def middle(length, leave, gbuf, wbuf, x_ref, smooth_ref, fwd, inv, tw_ref, out_ref, sbuf, send, recv, loc):
     fwd, inv = (fwd[0][...], fwd[1][...]), (inv[0][...], inv[1][...])
     radix = length // LANES
     h = radix // 2
@@ -249,14 +249,43 @@
             x, ix = wc * x - ws * ix, wc * ix + ws * x
         return jnp.concatenate([x, ix], axis=0)
 
+    width = smooth_ref[0]
+    scale = -2.0 * math.pi**2 * width * width
+    edge = -float(length // 2)
+
+    def weigh(k, g1):
+        fx = k + radix * row
+        kx = jnp.where(fx < length // 2, fx, fx - length).astype(jnp.float32)
+
+        def kernel(ky):
+            square = jnp.maximum(kx * kx + ky * ky, 1.0)
+            damp = jnp.exp(scale * ((kx / length) ** 2 + (ky / length) ** 2))
+            inverse = damp / square
+            return (kx * kx - ky * ky) * inverse, -2.0 * kx * ky * inverse, damp
+
+        kr, ki, _ = kernel(ky)
+        nr, ni, damp_n = kernel(edge)
+        last = fx == length // 2
+        nr = jnp.where(last, 0.0, nr)
+        ni_in = jnp.where(last, 0.0, ni)
+        w1r = jnp.where(packed, 0.5 * (kr + nr), kr)
+        w1i = jnp.where(packed, 0.5 * ni_in, jnp.where(last, ki, 0.0))
+        w2r = jnp.where(packed, 0.5 * (kr - nr), jnp.where(last, 0.0, -ki))
+        w2i = jnp.where(packed, -0.5 * ni_in, 0.0)
+        gbuf[k] = w1r * g1 + w1i * turn(g1, sign)
+        wbuf[k, 0] = w2r
+        wbuf[k, 1] = w2i
+        if k == 0:
+            wbuf[radix, 0] = jnp.where(packed & last & (lane >= half), -ni, 0.0)
+
     for copy in leave[0]:
         copy.wait()
     sums = cos_sin_sums([x_ref[n, 0] for n in range(radix)])
     for k in range(0, radix, 2):
         pair = jnp.concatenate([spectra(k, sums), spectra(k + 1, sums)], axis=1)
         got = mm(fwd, split_value(pair))
-        gbuf[k] = got[:, :LANES]
-        gbuf[k + 1] = got[:, LANES:]
+        weigh(k, got[:, :LANES])
+        weigh(k + 1, got[:, LANES:])
     for copy in leave[1]:
         copy.wait()
     one = [x_ref[n, 0] for n in range(radix)]
@@ -268,38 +297,16 @@
     corner = jnp.sum(total * alternate, axis=0, keepdims=True)
     two = [jnp.where(packed, -sign * a, b) for a, b in zip(one, two_raw)]
     sums = cos_sin_sums(two)
-    width = smooth_ref[0]
-    scale = -2.0 * math.pi**2 * width * width
-    edge = -float(length // 2)
     results = []
     for k in range(radix):
         wc, ws = tw_ref[:, k : k + 1], tw_ref[:, radix + k : radix + k + 1]
         if k % 2 == 0:
             pair = jnp.concatenate([spectra(k, sums), spectra(k + 1, sums)], axis=1)
             both = mm(fwd, split_value(pair))
-        g1, g2 = gbuf[k], both[:, LANES * (k % 2) : LANES * (k % 2 + 1)]
-        fx = k + radix * row
-        kx = jnp.where(fx < length // 2, fx, fx - length).astype(jnp.float32)
-
-        def kernel(ky):
-            square = jnp.maximum(kx * kx + ky * ky, 1.0)
-            damp = jnp.exp(scale * ((kx / length) ** 2 + (ky / length) ** 2))
-            inverse = damp / square
-            return (kx * kx - ky * ky) * inverse, -2.0 * kx * ky * inverse, damp
-
-        kr, ki, _ = kernel(ky)
-        nr, ni, damp_n = kernel(edge)
-        last = fx == length // 2
-        nr = jnp.where(last, 0.0, nr)
-        ni_in = jnp.where(last, 0.0, ni)
-        w1r = jnp.where(packed, 0.5 * (kr + nr), kr)
-        w1i = jnp.where(packed, 0.5 * ni_in, jnp.where(last, ki, 0.0))
-        w2r = jnp.where(packed, 0.5 * (kr - nr), jnp.where(last, 0.0, -ki))
-        w2i = jnp.where(packed, -0.5 * ni_in, 0.0)
-        z = w1r * g1 + w1i * turn(g1, sign) + w2r * g2 + w2i * turn(g2, sign)
+        g2 = both[:, LANES * (k % 2) : LANES * (k % 2 + 1)]
+        z = gbuf[k] + wbuf[k, 0] * g2 + wbuf[k, 1] * turn(g2, sign)
         if k == 0:
-            extra = jnp.where(packed & last & (lane >= half), -ni * corner, 0.0)
-            z = z + extra
+            z = z + wbuf[radix, 0] * corner
         iz = turn(z, sign)
         t = mm(inv, split_value(jnp.concatenate([z, iz], axis=0)))
         if k:
@@ -476,7 +483,7 @@
 
 def kernel(sizes, shear, smooth_ref, off_hbm, thr_ref, wide_hbm, thin_hbm,
            x_ref, rms_ref, high_ref, cnt_ref,
-           xbuf, sbuf, spec, gbuf, field, zbuf, wide, off_ref, table, thin, sq_ref, cnt_own,
+           xbuf, sbuf, spec, gbuf, wbuf, field, zbuf, wide, off_ref, table, thin, sq_ref, cnt_own,
            top_ref, bot_ref, above_ref, below_ref, slots,
            asend, arecv, bsend, brecv, csend, crecv, esend, erecv, hsend, hrecv, loc):
     nx, ny = sizes
@@ -498,7 +505,7 @@
     h = nx // LANES // 2
     tc, ts, tw = thin.at[0:h], thin.at[h : 2 * h], thin.at[2 * h : 2 * h + LANES]
     leave = forward_y(arrive, xbuf, ((t[0], t[1]), (t[2], t[3])), tc, ts, spec, sbuf, bsend, brecv, loc.at[pl.ds(5, 2)])
-    middle(nx, leave, gbuf, spec, smooth_ref, (t[8], t[9]), (t[10], t[11]), tw, zbuf, field, csend, crecv, loc.at[pl.ds(7, 1)])
+    middle(nx, leave, gbuf, wbuf, spec, smooth_ref, (t[8], t[9]), (t[10], t[11]), tw, zbuf, field, csend, crecv, loc.at[pl.ds(7, 1)])
     inverse_y(zbuf, ((t[4], t[5]), (t[6], t[7])), tc, ts, x_ref, sq_ref, top_ref, bot_ref)
     peaks(float(nx * ny), x_ref, sq_ref, top_ref, bot_ref, off_ref, thr_ref, rms_ref, high_ref, cnt_ref,
           cnt_own, wide, above_ref, below_ref, slots, esend, erecv, hsend, hrecv)
@@ -538,6 +545,7 @@
             vm(count, 2, rows, LANES),
             vm(count, 2, rows, LANES),
             vm(nx // LANES, LANES, LANES),
+            vm(nx // LANES + 1, 2, LANES, LANES),
             vm(count, rows, LANES),
             vm(count, rows, LANES),
             vm(rows + 16, ny),

time: 141 us -> 141 us (level)
  no operation moved by 1% of the time
where the time goes in v5:
time: 141 us
  Pallas kernels  135 us (96%)
  other arithmetic  2.87 us (2%)
    pallas_call x1, Pallas kernels, one_map(): pl.pallas_call(partial(kernel, (nx, ny)), out_shape=(shape(rows, ny), sha...  135 us
    another operation x1, other arithmetic, body(): return tuple((jnp.stack(parts) for parts in zip(*outs)))  2.87 us

profile of v5, /device:TPU:0, one launch (start us, length us, event | category | flops | bytes accessed | tf_op | source)
XLA Modules:
  0.0 140.7 jit_solution(13566759939677386730)
XLA Ops:
  1.3 135.4 %shard_map.130 = (f32[128,2048]{1,0:T(8,128)}, f32[1,128]{1,0:T(1,128)}, f32[8,128]{1,0:T(8,128)}, f32[1,128]{1,0:T(1,128)}) custom-call(f32[2,512,512]{2,1,0:T(8,128)} %bitcast.9, f32[1]{0:T(128)S(6)} %copy.16.smooth_ref, s32[8,128]{1,0:T(8,128)} %bitcast.10, s32[16]{0:T(128)} %bitcast.12, bf16[2560,256]{1,0:T(8,128)(2,1)} %constant.49.wide_hbm, ...), custom_call_target="tpu_custom_call" | custom-call | tf_op jit(solution)/shard_map/pallas_call | solution.py:538
  136.7 0.0 copy-start
  136.7 0.0 copy-start.1
  136.7 2.9 %divide_bitcast_fusion = f32[1,128,2048]{2,1,0:T(8,128)} fusion(f32[128,2048]{1,0:T(8,128)} %get-tuple-element.7, f32[]{:T(128)} %bitcast.13), kind=kLoop, calls=%fused_computation | loop fusion | flops 262144 | bytes 2097156 | tf_op jit(solution)/shard_map/stack | solution.py:573
  139.6 0.0 copy-done
  139.6 0.6 copy.17
  140.2 0.0 copy-done.1
  140.2 0.5 copy.18
Async XLA Ops:
  136.7 2.9 %copy-start = (f32[8,128]{1,0:T(8,128)S(1)}, f32[8,128]{1,0:T(8,128)}, u32[]{:S(2)}) copy-start(f32[8,128]{1,0:T(8,128)} %get-tuple-element.9) | copy-start | bytes 12292
  136.7 3.5 %copy-start.1 = (f32[1,128]{1,0:T(1,128)S(1)}, f32[1,128]{1,0:T(1,128)}, u32[]{:S(2)}) copy-start(f32[1,128]{1,0:T(1,128)} %get-tuple-element.10) | copy-start | bytes 1540
